TPU v7x, 256 devices: a whole 4x4x8 slice. The times are simulated.
256 devices in a mesh: section: 16 (over x, z_hi, core), rows: 16 (over y, z_lo).
Axes of the slice: x: 4, y: 4, z: 8 (z_hi: 2, z_lo: 4; z = z_hi * 4 + z_lo), core: 2. Of those that a mesh axis runs over, the one named last changes fastest.
Arguments:
- fwd_in: bfloat16 [16, 256, 32, 512], P('section', 'rows'), may hold values from -6 to 6
- grad_in: bfloat16 [16, 256, 32, 512], P('section', 'rows'), may hold values from -6 to 6
- saved_in: bfloat16 [16, 256, 32, 512], P('section', 'rows'), may hold values from -6 to 6
- mirror_held: bfloat16 [16, 256, 32, 512], P('section', 'rows'), may hold values from -6 to 6
- target: bfloat16 [256, 32, 512], P('rows'), may hold values from -6 to 6
- w_first: bfloat16 [16, 3, 3, 512, 512], P('section'), may hold values from -0.09375 to 0.09375
- w_second: bfloat16 [16, 3, 3, 512, 512], P('section'), may hold values from -0.09375 to 0.09375
Outputs:
- fwd_next: bfloat16 [16, 256, 32, 512], P('section', 'rows')
- grad_next: bfloat16 [16, 256, 32, 512], P('section', 'rows')
- mirror_next: bfloat16 [16, 256, 32, 512], P('section', 'rows')
All inputs are finite; a program needn't handle non-finite values.
Results may differ from a plain program's by a relative error of at most 0.0085.
Values may be sent and summed in bfloat16 or wider, within the bound.
No kernel may reach another device: no remote copies, remote signals or barrier semaphores. Data moves between devices by JAX's collectives and lax.ppermute only.
A program may use at most 64 MiB of HBM per device.

v0:
```python
import jax
import jax.numpy as jnp
from jax import lax
from jax.sharding import PartitionSpec as P


def extended(value, sides, width):
    for axis, dim in sides:
        count, length = (lax.axis_size(axis), value.shape[dim])
        up = [(i, (i + 1) % count) for i in range(count - 1)]
        down = [(j, i) for i, j in up]
        last = lax.slice_in_dim(value, length - width, length, axis=dim)
        leading = lax.slice_in_dim(value, 0, width, axis=dim)
        before = lax.ppermute(last, axis, up)
        after = lax.ppermute(leading, axis, down)
        value = jnp.concatenate([before, value, after], axis=dim)
    return value


def shifted(value, axis, by):
    count = lax.axis_size(axis)
    pairs = [(i, i + by) for i in range(count) if 0 <= i + by < count]
    return lax.ppermute(value, axis, pairs)


def partner(value, axis, distance):
    mask = 2**distance
    pairs = [(source, source ^ mask) for source in range(lax.axis_size(axis))]
    return lax.ppermute(value, axis, pairs)


def conv_rows(field, kernel):
    return lax.conv_general_dilated(
        field,
        kernel,
        (1, 1),
        ((0, 0), (1, 1)),
        dimension_numbers=("NHWC", "HWIO", "NHWC"),
        preferred_element_type=jnp.float32,
    )


def flipped(kernel):
    return jnp.transpose(kernel[::-1, ::-1], (0, 1, 3, 2))


def silu_slope(pre):
    sig = jax.nn.sigmoid(pre)
    return sig * (1.0 + pre * (1.0 - sig))


def double_rim(field):
    return extended(field, (("rows", 1),), 2)


def on_device(fwd_in, grad_in, saved_in, mirror_held, target, w_first, w_second):
    act = fwd_in[0]
    grad = grad_in[0]
    saved = saved_in[0]
    held = mirror_held[0]
    kern_one = w_first[0]
    kern_two = w_second[0]
    local_rows = act.shape[0]
    section = lax.axis_index("section")
    sections = lax.axis_size("section")
    decoder = (section >= sections // 2).astype(jnp.float32)
    is_last = section == sections - 1
    first_row = lax.axis_index("rows") * local_rows
    total_rows = local_rows * lax.axis_size("rows")
    global_row = first_row - 1 + jnp.arange(local_rows + 2, dtype=jnp.int32)
    inside = ((global_row >= 0) & (global_row < total_rows)).astype(jnp.float32)[:, None, None]
    flip_one = flipped(kern_one)
    flip_two = flipped(kern_two)
    block_in = act.astype(jnp.float32) + decoder * held.astype(jnp.float32)
    block_b = block_in.astype(jnp.bfloat16)
    padded = double_rim(block_b[None])
    hidden = (jax.nn.silu(conv_rows(padded, kern_one)[0]) * inside).astype(jnp.bfloat16)
    output = (block_in + conv_rows(hidden[None], kern_two)[0]).astype(jnp.bfloat16)
    g_top = jnp.where(
        is_last,
        output.astype(jnp.float32) - target.astype(jnp.float32),
        grad.astype(jnp.float32) + (1.0 - decoder) * held.astype(jnp.float32),
    ).astype(jnp.bfloat16)
    kept = jnp.where(is_last, block_b, saved)
    paired = jnp.stack([kept, g_top], axis=0)
    rimmed = double_rim(paired)
    pre = conv_rows(rimmed[0:1], kern_one)[0]
    back = conv_rows(rimmed[1:2], flip_two)[0]
    g_mid = (silu_slope(pre) * back * inside).astype(jnp.bfloat16)
    g_low = (g_top.astype(jnp.float32) + conv_rows(g_mid[None], flip_one)[0]).astype(jnp.bfloat16)
    fwd_next = shifted(output, "section", 1)
    grad_next = shifted(g_low, "section", -1)
    payload = jnp.where(section >= sections // 2, g_low, output)
    bit_count = sections.bit_length() - 1
    for bit in list(range(bit_count)):
        payload = partner(payload, "section", bit)
    return (fwd_next[None], grad_next[None], payload[None])


def solution(mesh):
    return jax.shard_map(
        on_device,
        mesh=mesh,
        in_specs=(
            P("section", "rows", None, None),
            P("section", "rows", None, None),
            P("section", "rows", None, None),
            P("section", "rows", None, None),
            P("rows", None, None),
            P("section", None, None, None, None),
            P("section", None, None, None, None),
        ),
        out_specs=(
            P("section", "rows", None, None),
            P("section", "rows", None, None),
            P("section", "rows", None, None),
        ),
        check_vma=False,
    )
```

profile of v0, /device:TPU:24, one launch (start us, length us, event | category | flops | bytes accessed | tf_op | source)
XLA Modules:
  0.0 120.2 jit_solution(15723959756671294314)
XLA Ops:
  0.6 2.2 %copy_select_fusion = (bf16[1,16,32,512]{3,1,2,0:T(8,128)(2,1)S(1)}, bf16[1,16,32,512]{3,1,2,0:T(8,128)(2,1)S(1)}) fusion(bf16[1,16,32,512]{3,2,1,0:T(8,128)(2,1)} %param.9, pred[]{:T(512)S(6)} %eq.3, bf16[1,16,32,512]{3,2,1,0:T(8,128)(2,1)} %param.10, f32[]{:T(128)S(6)} %convert_element_type.57, bf16[1,16,32,512]{3,2,1,0:T(8,128)(2,1)} %param.7), kind=kLoop, calls=%fused_computation.79 | loop fusion | flops 1572864 | bytes 2621445 | tf_op jit(solution)/shard_map/jit(_where)/select_n | solution.py:84
  2.9 0.1 fusion.109
  3.0 3.8 %collective-permute-start = (bf16[1,2,32,512]{3,1,2,0:T(2,128)(2,1)S(1)}, bf16[1,2,32,512]{3,1,2,0:T(2,128)(2,1)S(1)}, u32[]{:S(2)}, u32[]{:S(2)}) collective-permute-start(bf16[1,2,32,512]{3,1,2,0:T(2,128)(2,1)S(1)} %get-tuple-element.20), channel_id=1, source_target_pairs={{0,1},{1,2},{2,3},{3,4},{4,5},{5,6},{6,7},{7,8},{8,9},{9,10},{10,1... | collective-permute-start | bytes 196616 | tf_op jit(solution)/shard_map/ppermute | solution.py:14
  6.8 4.8 %collective-permute-start.1 = (bf16[1,2,32,512]{3,1,2,0:T(2,128)(2,1)S(1)}, bf16[1,2,32,512]{3,1,2,0:T(2,128)(2,1)S(1)}, u32[]{:S(2)}, u32[]{:S(2)}) collective-permute-start(bf16[1,2,32,512]{3,1,2,0:T(2,128)(2,1)S(1)} %get-tuple-element.21), channel_id=1, source_target_pairs={{1,0},{2,1},{3,2},{4,3},{5,4},{6,5},{7,6},{8,7},{9,8},{10,9},{11,1... | collective-permute-start | bytes 196616 | tf_op jit(solution)/shard_map/ppermute | solution.py:15
  11.7 0.4 collective-permute-done
  12.0 1.5 %collective-permute-done.1 = bf16[1,2,32,512]{3,1,2,0:T(2,128)(2,1)S(1)} collective-permute-done((bf16[1,2,32,512]{3,1,2,0:T(2,128)(2,1)S(1)}, bf16[1,2,32,512]{3,1,2,0:T(2,128)(2,1)S(1)}, u32[]{:S(2)}, u32[]{:S(2)}) %collective-permute-start.1) | collective-permute-done | bytes 65568 | tf_op jit(solution)/shard_map/ppermute | solution.py:15
  13.5 0.4 maximum_bitcast_fusion
  14.0 0.1 pad
  14.0 0.2 copy.13
  14.3 0.1 slice.35
  14.4 1.5 %copy-done.4 = bf16[1,3,3,512,512]{4,3,2,1,0:T(8,128)(2,1)S(1)} copy-done((bf16[1,3,3,512,512]{4,3,2,1,0:T(8,128)(2,1)S(1)}, bf16[1,3,3,512,512]{4,3,2,1,0:T(8,128)(2,1)}, u32[]{:S(2)}) %copy-start.4) | copy-done | bytes 4718616
  15.9 3.9 %fusion.30 = bf16[18,1,8,5,512]{4,2,3,0,1:T(8,128)(2,1)S(1)} fusion(bf16[1,3,3,512,512]{4,3,2,1,0:T(8,128)(2,1)S(1)} %copy-done.4, bf16[20,1,7,2,512]{4,2,3,0,1:T(8,128)(2,1)S(1)} %slice.35, bf16[20,1,8,5,512]{4,2,3,0,1:T(8,128)(2,1)S(1)} %copy.13, f32[18]{0:T(128)S(1)} %and_convert_fusion, pred[8,5]{0,1:T(8,128)(4,1)S(1)} %copy-done.5), kind=kOutput, calls=%fused_computation.28 | convolution fusion | flops 3403776000 | bytes 6561904 | tf_op jit(solution)/shard_map/conv_general_dilated | solution.py:33
  19.8 3.2 %fusion.2 = f32[16,8,5,512]{3,1,2,0:T(8,128)S(1)} fusion(bf16[1,3,3,512,512]{4,3,2,1,0:T(8,128)(2,1)S(1)} %bitcast.94, bf16[18,1,7,1,512]{4,2,3,0,1:T(8,128)(2,1)S(1)} %get-tuple-element.19, bf16[18,1,7,1,512]{4,2,3,0,1:T(8,128)(2,1)S(1)} %get-tuple-element.18, bf16[18,1,8,5,512]{4,2,3,0,1:T(8,128)(2,1)S(1)} %fusion.30), kind=kOutput, calls=%fused_computation.2 | convolution fusion | flops 3025059840 | bytes 7024640 | tf_op jit(solution)/shard_map/conv_general_dilated | solution.py:33
  23.1 0.8 copy.14
  23.9 0.2 copy-done
  24.1 0.2 copy-done.1
  24.3 0.2 copy-done.2
  24.4 0.2 copy-done.3
  24.6 1.4 %fusion.55 = (bf16[16,32,512]{2,0,1:T(8,128)(2,1)S(1)}, bf16[16,32,512]{2,0,1:T(8,128)(2,1)S(1)}) fusion(bf16[1,16,32,512]{3,2,1,0:T(8,128)(2,1)S(1)} %copy-done.2, bf16[16,32,512]{2,1,0:T(8,128)(2,1)S(1)} %copy-done.3, f32[]{:T(128)S(6)} %sub.15, pred[]{:T(512)S(6)} %eq.3, bf16[1,16,32,512]{3,2,1,0:T(8,128)(2,1)S(1)} %copy-done, ...), kind=kLoop, calls=%fused_computation.48 | loop fusion | flops 3670016 | bytes 4194313 | tf_op jit(solution)/shard_map/convert_element_type | solution.py:83
  26.0 0.2 pad_maximum_fusion.2
  26.2 3.3 %collective-permute-start.3 = (bf16[2,2,32,512]{3,1,2,0:T(2,128)(2,1)S(1)}, bf16[2,2,32,512]{3,1,2,0:T(2,128)(2,1)S(1)}, u32[]{:S(2)}, u32[]{:S(2)}) collective-permute-start(bf16[2,2,32,512]{3,1,2,0:T(2,128)(2,1)S(1)} %get-tuple-element.14), channel_id=1, source_target_pairs={{0,1},{1,2},{2,3},{3,4},{4,5},{5,6},{6,7},{7,8},{8,9},{9,10},{10,1... | collective-permute-start | bytes 393224 | tf_op jit(solution)/shard_map/ppermute | solution.py:14
  29.5 5.8 %collective-permute-start.4 = (bf16[2,2,32,512]{3,1,2,0:T(2,128)(2,1)S(1)}, bf16[2,2,32,512]{3,1,2,0:T(2,128)(2,1)S(1)}, u32[]{:S(2)}, u32[]{:S(2)}) collective-permute-start(bf16[2,2,32,512]{3,1,2,0:T(2,128)(2,1)S(1)} %get-tuple-element.15), channel_id=1, source_target_pairs={{1,0},{2,1},{3,2},{4,3},{5,4},{6,5},{7,6},{8,7},{9,8},{10,9},{11,1... | collective-permute-start | bytes 393224 | tf_op jit(solution)/shard_map/ppermute | solution.py:15
  35.3 0.9 collective-permute-done.3
  36.2 1.4 %collective-permute-done.4 = bf16[2,2,32,512]{3,1,2,0:T(2,128)(2,1)S(1)} collective-permute-done((bf16[2,2,32,512]{3,1,2,0:T(2,128)(2,1)S(1)}, bf16[2,2,32,512]{3,1,2,0:T(2,128)(2,1)S(1)}, u32[]{:S(2)}, u32[]{:S(2)}) %collective-permute-start.4) | collective-permute-done | bytes 131104 | tf_op jit(solution)/shard_map/ppermute | solution.py:15
  37.6 1.1 pad_maximum_fusion
  38.7 0.1 slice_bitcast_fusion.3
  38.8 0.1 pad.6
  38.9 0.2 copy.21
  39.2 0.1 slice.42
  39.2 3.7 %fusion = f32[18,8,5,512]{3,1,2,0:T(8,128)S(1)} fusion(bf16[1,3,3,512,512]{4,3,2,1,0:T(8,128)(2,1)S(1)} %bitcast.94, bf16[20,1,7,2,512]{4,2,3,0,1:T(8,128)(2,1)S(1)} %slice.42, bf16[20,1,8,5,512]{4,2,3,0,1:T(8,128)(2,1)S(1)} %copy.21), kind=kOutput, calls=%fused_computation | convolution fusion | flops 3400826880 | bytes 7299072 | tf_op jit(solution)/shard_map/conv_general_dilated | solution.py:33
  43.0 0.2 copy.19
  43.3 0.1 slice.40
  43.3 4.1 %fusion.27 = bf16[18,1,8,5,512]{4,2,3,0,1:T(8,128)(2,1)S(1)} fusion(f32[18,8,5,512]{3,1,2,0:T(8,128)S(1)} %fusion, bf16[1,3,3,512,512]{4,3,2,1,0:T(8,128)(2,1)S(1)} %copy-done.4, bf16[20,1,7,2,512]{4,2,3,0,1:T(8,128)(2,1)S(1)} %slice.40, bf16[20,1,8,5,512]{4,2,3,0,1:T(8,128)(2,1)S(1)} %copy.19, f32[18]{0:T(128)S(1)} %and_convert_fusion, ...), kind=kOutput, calls=%fused_computation.27 | convolution fusion | flops 3405619200 | bytes 8036464 | tf_op jit(solution)/shard_map/conv_general_dilated | solution.py:33
  47.5 3.3 %fusion.4 = f32[16,8,5,512]{3,1,2,0:T(8,128)S(1)} fusion(bf16[1,3,3,512,512]{4,3,2,1,0:T(8,128)(2,1)S(1)} %copy-done.4, bf16[18,1,7,1,512]{4,2,3,0,1:T(8,128)(2,1)S(1)} %get-tuple-element.17, bf16[18,1,7,1,512]{4,2,3,0,1:T(8,128)(2,1)S(1)} %get-tuple-element.16, bf16[18,1,8,5,512]{4,2,3,0,1:T(8,128)(2,1)S(1)} %fusion.27), kind=kOutput, calls=%fused_computation.4 | convolution fusion | flops 3025059840 | bytes 7024640 | tf_op jit(solution)/shard_map/conv_general_dilated | solution.py:33
  50.8 0.8 copy.22
  51.6 0.6 broadcast_select_fusion
  52.1 0.1 collective-permute-start.6
  52.2 1.9 %collective-permute-done.6 = bf16[16,32,512]{2,0,1:T(8,128)(2,1)S(1)} collective-permute-done((bf16[16,32,512]{2,0,1:T(8,128)(2,1)S(1)}, bf16[16,32,512]{2,0,1:T(8,128)(2,1)S(1)}, u32[]{:S(2)}, u32[]{:S(2)}) %collective-permute-start.6) | collective-permute-done | bytes 524320 | tf_op jit(solution)/shard_map/ppermute | solution.py:29
  54.1 7.1 %collective-permute-start.7 = (bf16[16,32,512]{2,0,1:T(8,128)(2,1)S(1)}, bf16[16,32,512]{2,0,1:T(8,128)(2,1)S(1)}, u32[]{:S(2)}, u32[]{:S(2)}) collective-permute-start(bf16[16,32,512]{2,0,1:T(8,128)(2,1)S(1)} %collective-permute-done.6), channel_id=1, source_target_pairs={{0,32},{16,48},{32,0},{48,16},{64,96},{80,112},{96,64},{112,80},{1... | collective-permute-start | bytes 1572872 | tf_op jit(solution)/shard_map/ppermute | solution.py:29
  61.2 23.6 %collective-permute-done.7 = bf16[16,32,512]{2,0,1:T(8,128)(2,1)S(1)} collective-permute-done((bf16[16,32,512]{2,0,1:T(8,128)(2,1)S(1)}, bf16[16,32,512]{2,0,1:T(8,128)(2,1)S(1)}, u32[]{:S(2)}, u32[]{:S(2)}) %collective-permute-start.7) | collective-permute-done | bytes 524320 | tf_op jit(solution)/shard_map/ppermute | solution.py:29
  84.8 1.5 %collective-permute-start.8 = (bf16[16,32,512]{2,0,1:T(8,128)(2,1)S(1)}, bf16[16,32,512]{2,0,1:T(8,128)(2,1)S(1)}, u32[]{:S(2)}, u32[]{:S(2)}) collective-permute-start(bf16[16,32,512]{2,0,1:T(8,128)(2,1)S(1)} %collective-permute-done.7), channel_id=1, source_target_pairs={{0,64},{16,80},{32,96},{48,112},{64,0},{80,16},{96,32},{112,48},{1... | collective-permute-start | bytes 1572872 | tf_op jit(solution)/shard_map/ppermute | solution.py:29
  86.3 1.4 %collective-permute-start.2 = (bf16[16,32,512]{2,0,1:T(8,128)(2,1)S(1)}, bf16[16,32,512]{2,0,1:T(8,128)(2,1)S(1)}, u32[]{:S(2)}, u32[]{:S(2)}) collective-permute-start(bf16[16,32,512]{2,0,1:T(8,128)(2,1)S(1)} %get-tuple-element.11), channel_id=1, source_target_pairs={{0,16},{16,32},{32,48},{48,64},{64,80},{80,96},{96,112},{112,128},... | collective-permute-start | bytes 1572872 | tf_op jit(solution)/shard_map/ppermute | solution.py:23
  87.7 1.3 %collective-permute-start.5 = (bf16[16,32,512]{2,0,1:T(8,128)(2,1)S(1)}, bf16[16,32,512]{2,0,1:T(8,128)(2,1)S(1)}, u32[]{:S(2)}, u32[]{:S(2)}) collective-permute-start(bf16[16,32,512]{2,0,1:T(8,128)(2,1)S(1)} %get-tuple-element.7), channel_id=1, source_target_pairs={{16,0},{32,16},{48,32},{64,48},{80,64},{96,80},{112,96},{128,112},... | collective-permute-start | bytes 1572872 | tf_op jit(solution)/shard_map/ppermute | solution.py:23
  89.0 14.9 %collective-permute-done.8 = bf16[16,32,512]{2,0,1:T(8,128)(2,1)S(1)} collective-permute-done((bf16[16,32,512]{2,0,1:T(8,128)(2,1)S(1)}, bf16[16,32,512]{2,0,1:T(8,128)(2,1)S(1)}, u32[]{:S(2)}, u32[]{:S(2)}) %collective-permute-start.8) | collective-permute-done | bytes 524320 | tf_op jit(solution)/shard_map/ppermute | solution.py:29
  103.9 1.1 copy.23
  105.0 1.1 copy.24
  106.1 13.1 %collective-permute-done.9 = bf16[16,32,512]{2,0,1:T(8,128)(2,1)S(1)} collective-permute-done((bf16[16,32,512]{2,0,1:T(8,128)(2,1)S(1)}, bf16[16,32,512]{2,0,1:T(8,128)(2,1)S(1)}, u32[]{:S(2)}, u32[]{:S(2)}) %collective-permute-start.9) | collective-permute-done | bytes 524320 | tf_op jit(solution)/shard_map/ppermute | solution.py:29
  119.2 1.1 copy.25
  (19 shorter events, 0.2 us)
Async XLA Ops:
  3.0 9.1 %collective-permute-start = (bf16[1,2,32,512]{3,1,2,0:T(2,128)(2,1)S(1)}, bf16[1,2,32,512]{3,1,2,0:T(2,128)(2,1)S(1)}, u32[]{:S(2)}, u32[]{:S(2)}) collective-permute-start(bf16[1,2,32,512]{3,1,2,0:T(2,128)(2,1)S(1)} %get-tuple-element.20), channel_id=1, source_target_pairs={{0,1},{1,2},{2,3},{3,4},{4,5},{5,6},{6,7},{7,8},{8,9},{9,10},{10,1... | collective-permute-start | bytes 196616 | tf_op jit(solution)/shard_map/ppermute | solution.py:14
  6.8 6.7 %collective-permute-start.1 = (bf16[1,2,32,512]{3,1,2,0:T(2,128)(2,1)S(1)}, bf16[1,2,32,512]{3,1,2,0:T(2,128)(2,1)S(1)}, u32[]{:S(2)}, u32[]{:S(2)}) collective-permute-start(bf16[1,2,32,512]{3,1,2,0:T(2,128)(2,1)S(1)} %get-tuple-element.21), channel_id=1, source_target_pairs={{1,0},{2,1},{3,2},{4,3},{5,4},{6,5},{7,6},{8,7},{9,8},{10,9},{11,1... | collective-permute-start | bytes 196616 | tf_op jit(solution)/shard_map/ppermute | solution.py:15
  13.5 2.3 %copy-start.4 = (bf16[1,3,3,512,512]{4,3,2,1,0:T(8,128)(2,1)S(1)}, bf16[1,3,3,512,512]{4,3,2,1,0:T(8,128)(2,1)}, u32[]{:S(2)}) copy-start(bf16[1,3,3,512,512]{4,3,2,1,0:T(8,128)(2,1)} %param.12) | copy-start | bytes 14155780
  14.0 1.8 %copy-start.5 = (pred[8,5]{0,1:T(8,128)(4,1)S(1)}, pred[8,5]{0,1:T(8,128)(4,1)}, u32[]{:S(2)}) copy-start(pred[8,5]{0,1:T(8,128)(4,1)} %constant.49) | copy-start | bytes 124
  14.3 5.5 %slice-start = ((s8[4718592]{0:T(1024)(128)(4,1)}), s8[4194304]{0:T(1024)(128)(4,1)S(1)}, s32[]{:S(2)}) async-start(s8[4718592]{0:T(1024)(128)(4,1)} %bitcast.93), calls=%async_computation | async-start | bytes 8388608
  15.9 3.9 %slice-start.1 = ((s8[4718592]{0:T(1024)(128)(4,1)}), s8[524288]{0:T(1024)(128)(4,1)S(1)}, s32[]{:S(2)}) async-start(s8[4718592]{0:T(1024)(128)(4,1)} %bitcast.93), calls=%async_computation.1 | async-start | bytes 1048576
  23.1 1.0 copy-start
  23.1 1.2 copy-start.1
  23.1 1.3 %copy-start.2 = (bf16[1,16,32,512]{3,2,1,0:T(8,128)(2,1)S(1)}, bf16[1,16,32,512]{3,2,1,0:T(8,128)(2,1)}, u32[]{:S(2)}) copy-start(bf16[1,16,32,512]{3,2,1,0:T(8,128)(2,1)} %param.8) | copy-start | bytes 1572868
  23.1 1.5 %copy-start.3 = (bf16[16,32,512]{2,1,0:T(8,128)(2,1)S(1)}, bf16[16,32,512]{2,1,0:T(8,128)(2,1)}, u32[]{:S(2)}) copy-start(bf16[16,32,512]{2,1,0:T(8,128)(2,1)} %param.11) | copy-start | bytes 1572868
  26.2 10.0 %collective-permute-start.3 = (bf16[2,2,32,512]{3,1,2,0:T(2,128)(2,1)S(1)}, bf16[2,2,32,512]{3,1,2,0:T(2,128)(2,1)S(1)}, u32[]{:S(2)}, u32[]{:S(2)}) collective-permute-start(bf16[2,2,32,512]{3,1,2,0:T(2,128)(2,1)S(1)} %get-tuple-element.14), channel_id=1, source_target_pairs={{0,1},{1,2},{2,3},{3,4},{4,5},{5,6},{6,7},{7,8},{8,9},{9,10},{10,1... | collective-permute-start | bytes 393224 | tf_op jit(solution)/shard_map/ppermute | solution.py:14
  29.5 8.1 %collective-permute-start.4 = (bf16[2,2,32,512]{3,1,2,0:T(2,128)(2,1)S(1)}, bf16[2,2,32,512]{3,1,2,0:T(2,128)(2,1)S(1)}, u32[]{:S(2)}, u32[]{:S(2)}) collective-permute-start(bf16[2,2,32,512]{3,1,2,0:T(2,128)(2,1)S(1)} %get-tuple-element.15), channel_id=1, source_target_pairs={{1,0},{2,1},{3,2},{4,3},{5,4},{6,5},{7,6},{8,7},{9,8},{10,9},{11,1... | collective-permute-start | bytes 393224 | tf_op jit(solution)/shard_map/ppermute | solution.py:15
  52.1 2.0 %collective-permute-start.6 = (bf16[16,32,512]{2,0,1:T(8,128)(2,1)S(1)}, bf16[16,32,512]{2,0,1:T(8,128)(2,1)S(1)}, u32[]{:S(2)}, u32[]{:S(2)}) collective-permute-start(bf16[16,32,512]{2,0,1:T(8,128)(2,1)S(1)} %get-tuple-element.6), channel_id=1, source_target_pairs={{0,16},{16,0},{32,48},{48,32},{64,80},{80,64},{96,112},{112,96},{1... | collective-permute-start | bytes 1572872 | tf_op jit(solution)/shard_map/ppermute | solution.py:29
  54.1 30.7 %collective-permute-start.7 = (bf16[16,32,512]{2,0,1:T(8,128)(2,1)S(1)}, bf16[16,32,512]{2,0,1:T(8,128)(2,1)S(1)}, u32[]{:S(2)}, u32[]{:S(2)}) collective-permute-start(bf16[16,32,512]{2,0,1:T(8,128)(2,1)S(1)} %collective-permute-done.6), channel_id=1, source_target_pairs={{0,32},{16,48},{32,0},{48,16},{64,96},{80,112},{96,64},{112,80},{1... | collective-permute-start | bytes 1572872 | tf_op jit(solution)/shard_map/ppermute | solution.py:29
  84.8 19.1 %collective-permute-start.8 = (bf16[16,32,512]{2,0,1:T(8,128)(2,1)S(1)}, bf16[16,32,512]{2,0,1:T(8,128)(2,1)S(1)}, u32[]{:S(2)}, u32[]{:S(2)}) collective-permute-start(bf16[16,32,512]{2,0,1:T(8,128)(2,1)S(1)} %collective-permute-done.7), channel_id=1, source_target_pairs={{0,64},{16,80},{32,96},{48,112},{64,0},{80,16},{96,32},{112,48},{1... | collective-permute-start | bytes 1572872 | tf_op jit(solution)/shard_map/ppermute | solution.py:29
  86.3 17.6 %collective-permute-start.2 = (bf16[16,32,512]{2,0,1:T(8,128)(2,1)S(1)}, bf16[16,32,512]{2,0,1:T(8,128)(2,1)S(1)}, u32[]{:S(2)}, u32[]{:S(2)}) collective-permute-start(bf16[16,32,512]{2,0,1:T(8,128)(2,1)S(1)} %get-tuple-element.11), channel_id=1, source_target_pairs={{0,16},{16,32},{32,48},{48,64},{64,80},{80,96},{96,112},{112,128},... | collective-permute-start | bytes 1572872 | tf_op jit(solution)/shard_map/ppermute | solution.py:23
  87.7 17.3 %collective-permute-start.5 = (bf16[16,32,512]{2,0,1:T(8,128)(2,1)S(1)}, bf16[16,32,512]{2,0,1:T(8,128)(2,1)S(1)}, u32[]{:S(2)}, u32[]{:S(2)}) collective-permute-start(bf16[16,32,512]{2,0,1:T(8,128)(2,1)S(1)} %get-tuple-element.7), channel_id=1, source_target_pairs={{16,0},{32,16},{48,32},{64,48},{80,64},{96,80},{112,96},{128,112},... | collective-permute-start | bytes 1572872 | tf_op jit(solution)/shard_map/ppermute | solution.py:23
  103.9 15.3 %collective-permute-start.9 = (bf16[16,32,512]{2,0,1:T(8,128)(2,1)S(1)}, bf16[16,32,512]{2,0,1:T(8,128)(2,1)S(1)}, u32[]{:S(2)}, u32[]{:S(2)}) collective-permute-start(bf16[16,32,512]{2,0,1:T(8,128)(2,1)S(1)} %collective-permute-done.8), channel_id=1, source_target_pairs={{0,128},{16,144},{32,160},{48,176},{64,192},{80,208},{96,224},{112... | collective-permute-start | bytes 1572872 | tf_op jit(solution)/shard_map/ppermute | solution.py:29
where the time goes:
time: 121 us; the launch traced here: 120 us
  waiting for transfers between devices  57.6 us (48%)
  starting transfers between devices  29.1 us (24%)
  matrix products  18.2 us (15%)
  local copies, waits for them, and re-layouts  8.46 us (7%)
  other arithmetic  5.94 us (5%)
    ppermute x4, waiting for transfers between devices, partner(): return lax.ppermute(value, axis, pairs)  53.4 us
    conv_general_dilated x5, matrix products, conv_rows(): lax.conv_general_dilated(field, kernel, (1, 1), ((0, 0), (1, 1)), dimensi...  18.2 us
    ppermute x2, starting transfers between devices, extended(): after = lax.ppermute(leading, axis, down)  10.6 us
    ppermute x4, starting transfers between devices, partner(): return lax.ppermute(value, axis, pairs)  8.73 us
    ppermute x2, starting transfers between devices, extended(): before = lax.ppermute(last, axis, up)  7.11 us
    unnamed x19, local copies, waits for them, and re-layouts  5.47 us
    ppermute x2, waiting for transfers between devices, extended(): after = lax.ppermute(leading, axis, down)  2.88 us
    ppermute x2, starting transfers between devices, shifted(): return lax.ppermute(value, axis, pairs)  2.67 us
  transfers between devices with their start and end apart: 10, of which 8 were waited for; matrix products, arithmetic and copies ran while one was open for 2% of the time, Pallas kernels for 0%

commit v1 on v0

v1 whole, which is shorter than its diff:
```python
import functools

import jax
import jax.numpy as jnp
from jax import lax
from jax.experimental import pallas as pl
from jax.experimental.pallas import tpu as pltpu
from jax.sharding import PartitionSpec as P

BF16 = jnp.bfloat16
F32 = jnp.float32
NN = (((1,), (0,)), ((), ()))
NT = (((1,), (1,)), ((), ()))
MIB = 1 << 20


class Sizes:
    def __init__(self, rows, cols, chan):
        self.rows, self.cols, self.chan = rows, cols, chan


def roles():
    section = lax.axis_index("section")
    sections = lax.axis_size("section")
    row = lax.axis_index("rows")
    decoder = section >= sections // 2
    last = section == sections - 1
    top = row == 0
    bottom = row == lax.axis_size("rows") - 1
    return section, decoder, last, top, bottom


def silu(v):
    return v * jax.nn.sigmoid(v)


def silu_slope(pre):
    sig = jax.nn.sigmoid(pre)
    return sig * (1.0 + pre * (1.0 - sig))


def spread(z, x3, row, value):
    cols, chan = z.cols, z.chan
    count = value.shape[0] // cols
    wide = value.astype(F32).reshape(count, cols, chan)
    col = lax.broadcasted_iota(jnp.int32, wide.shape, 1)
    before = jnp.where(col == 0, 0.0, pltpu.roll(wide, 1, 1))
    after = jnp.where(col == cols - 1, 0.0, pltpu.roll(wide, cols - 1, 1))
    at = slice(row * cols, (row + count) * cols)
    x3[at, 0:chan] = before.reshape(count * cols, chan).astype(BF16)
    x3[at, chan : 2 * chan] = value.astype(BF16)
    x3[at, 2 * chan :] = after.reshape(count * cols, chan).astype(BF16)


def conv(z, x3, pieces, w, acc, flip):
    cols, chan = z.cols, z.chan
    size = sum(n for _, n in pieces) * cols

    def left(a, lanes):
        parts = []
        for start, n in pieces:
            first = (start + a) * cols
            if not isinstance(a, int):
                first = pl.multiple_of(first, cols)
            parts.append(x3[pl.ds(first, n * cols), lanes])
        return parts[0] if len(parts) == 1 else jnp.concatenate(parts, 0)

    def tap_row(a):
        if not flip:
            right = w[pl.ds(3 * a, 3)].reshape(3 * chan, chan)
            return lax.dot_general(left(a, slice(None)), right, NN, preferred_element_type=F32)
        total = None
        for b in range(3):
            right = w[3 * (2 - a) + 2 - b]
            part = lax.dot_general(left(a, slice(b * chan, (b + 1) * chan)), right, NT, preferred_element_type=F32)
            total = part if total is None else total + part
        return total

    for a in range(3):
        if a == 0:
            acc[0:size] = tap_row(0)
        else:
            acc[0:size] += tap_row(a)


def block_input(fwd, held, decoder):
    return fwd.astype(F32) + decoder.astype(F32) * held.astype(F32)


def block_grad(grad, held, decoder):
    return (grad.astype(F32) + (1.0 - decoder.astype(F32)) * held.astype(F32)).astype(BF16)


def halo_body(z, fwd, grad, saved, held, target, up_ref, down_ref, buf, sem):
    rows, cols = z.rows, z.cols
    _, decoder, last, _, _ = roles()
    edge = 4 * cols
    copies = []
    for i, ref in enumerate((fwd, grad, saved, held, target)):
        for e, start in enumerate((0, (rows - 4) * cols)):
            copies.append(pltpu.make_async_copy(ref.at[pl.ds(start, edge)], buf.at[i, e], sem.at[i, e]))
    for c in copies:
        c.start()
    for c in copies:
        c.wait()
    two = 2 * cols
    for e, ref in enumerate((up_ref, down_ref)):
        near = slice(0, two) if e == 0 else slice(two, edge)
        u = block_input(buf[0, e], buf[3, e], decoder).astype(BF16)
        g = block_grad(buf[1, e], buf[3, e], decoder)
        kept = buf[2, e]

        @pl.when(last)
        def _():
            ref[0:edge] = u
            ref[edge:] = buf[4, e][near]

        @pl.when(jnp.logical_not(last))
        def _():
            ref[0:two] = u[near]
            ref[two:edge] = kept[near]
            ref[edge:] = g[near]


def inner_body(z, fwd, grad, saved, held, w1, w2, main_ref, mid_ref, x3, acc, pre):
    rows, cols = z.rows, z.cols
    _, decoder, last, _, _ = roles()
    backward = jnp.logical_and(decoder, jnp.logical_not(last))
    m1, m2 = (rows - 2) * cols, (rows - 4) * cols

    @pl.when(jnp.logical_not(backward))
    def _():
        u = block_input(fwd[...], held[...], decoder)
        spread(z, x3, 0, u.astype(BF16))
        conv(z, x3, [(0, rows - 2)], w1, acc, False)
        mid = silu(acc[0:m1]).astype(BF16)
        mid_ref[...] = mid
        spread(z, x3, 0, mid)
        conv(z, x3, [(0, rows - 4)], w2, acc, False)
        keep = slice(2 * cols, (rows - 2) * cols)
        main_ref[...] = (block_input(fwd[keep], held[keep], decoder) + acc[0:m2]).astype(BF16)

    @pl.when(backward)
    def _():
        spread(z, x3, 0, saved[...])
        conv(z, x3, [(0, rows - 2)], w1, acc, False)
        pre[0:m1] = acc[0:m1]
        spread(z, x3, 0, block_grad(grad[...], held[...], decoder))
        conv(z, x3, [(0, rows - 2)], w2, acc, True)
        mid = (silu_slope(pre[0:m1]) * acc[0:m1]).astype(BF16)
        mid_ref[...] = mid
        spread(z, x3, 0, mid)
        conv(z, x3, [(0, rows - 4)], w1, acc, True)
        keep = slice(2 * cols, (rows - 2) * cols)
        g = block_grad(grad[keep], held[keep], decoder)
        main_ref[...] = (g.astype(F32) + acc[0:m2]).astype(BF16)


def zero_rows(z, value, lo, hi, top, bottom):
    cols = z.cols
    place = lax.broadcasted_iota(jnp.int32, value.shape, 0)
    outside = jnp.logical_or(
        jnp.logical_and(top, place < lo * cols),
        jnp.logical_and(bottom, place >= value.shape[0] - hi * cols),
    )
    return jnp.where(outside, jnp.zeros_like(value), value)


def whole_backward(z, kept, top_grad, w1, w2, x3, acc, pre, out_ref, top, bottom):
    rows, cols = z.rows, z.cols
    m1, m2 = (rows + 2) * cols, rows * cols
    spread(z, x3, 0, kept[...])
    conv(z, x3, [(0, rows + 2)], w1, acc, False)
    pre[0:m1] = acc[0:m1]
    spread(z, x3, 0, top_grad[...])
    conv(z, x3, [(0, rows + 2)], w2, acc, True)
    mid = (silu_slope(pre[0:m1]) * acc[0:m1]).astype(BF16)
    spread(z, x3, 0, zero_rows(z, mid, 1, 1, top, bottom))
    conv(z, x3, [(0, rows)], w1, acc, True)
    out_ref[...] = (top_grad[2 * cols : 2 * cols + m2].astype(F32) + acc[0:m2]).astype(BF16)


def edge_body(z, fwd, grad, saved, held, target, above, below, w1, w2, inner, mid_in, out_ref, x3, acc, pre, kept, top_grad):
    rows, cols = z.rows, z.cols
    two, four, six = 2 * cols, 4 * cols, 6 * cols
    full = rows * cols
    _, decoder, last, top, bottom = roles()
    encoder = jnp.logical_not(decoder)
    m1 = (rows - 2) * cols

    def place_inner():
        out_ref[two : full - two] = inner[...]

    @pl.when(encoder)
    def _():
        place_inner()
        u = block_input(fwd[...], held[...], decoder).astype(BF16)
        spread(z, x3, 0, jnp.concatenate([above[0:two], u[0:two], u[full - two :], below[0:two]], 0))
        conv(z, x3, [(0, 2), (4, 2)], w1, acc, False)
        mid = zero_rows(z, silu(acc[0:four]).astype(BF16), 1, 1, top, bottom)
        spread(z, x3, 0, jnp.concatenate([mid[0:two], mid_in[0:two], mid_in[m1 - two :], mid[two:]], 0))
        conv(z, x3, [(0, 2), (4, 2)], w2, acc, False)
        out_ref[0:two] = (block_input(fwd[0:two], held[0:two], decoder) + acc[0:two]).astype(BF16)
        at = slice(full - two, full)
        out_ref[at] = (block_input(fwd[at], held[at], decoder) + acc[two:four]).astype(BF16)

    @pl.when(jnp.logical_and(decoder, jnp.logical_not(last)))
    def _():
        place_inner()
        at = slice(full - two, full)
        spread(z, x3, 0, jnp.concatenate([above[two:four], saved[0:two], saved[at], below[two:four]], 0))
        conv(z, x3, [(0, 2), (4, 2)], w1, acc, False)
        pre[0:four] = acc[0:four]
        g_low = block_grad(grad[0:two], held[0:two], decoder)
        g_high = block_grad(grad[at], held[at], decoder)
        spread(z, x3, 0, jnp.concatenate([above[four:six], g_low, g_high, below[four:six]], 0))
        conv(z, x3, [(0, 2), (4, 2)], w2, acc, True)
        mid = (silu_slope(pre[0:four]) * acc[0:four]).astype(BF16)
        mid = zero_rows(z, mid, 1, 1, top, bottom)
        spread(z, x3, 0, jnp.concatenate([mid[0:two], mid_in[0:two], mid_in[m1 - two :], mid[two:]], 0))
        conv(z, x3, [(0, 2), (4, 2)], w1, acc, True)
        out_ref[0:two] = (g_low.astype(F32) + acc[0:two]).astype(BF16)
        out_ref[at] = (g_high.astype(F32) + acc[two:four]).astype(BF16)

    @pl.when(last)
    def _():
        eight = 8 * cols
        u = block_input(fwd[...], held[...], decoder)
        ub = u.astype(BF16)
        spread(z, x3, 0, jnp.concatenate([above[0:four], ub[0:two], ub[full - two :], below[0:four]], 0))
        conv(z, x3, [(0, 4), (6, 4)], w1, acc, False)
        mid = zero_rows(z, silu(acc[0:eight]).astype(BF16), 3, 3, top, bottom)
        spread(z, x3, 0, jnp.concatenate([mid[0:four], mid_in[0:two], mid_in[m1 - two :], mid[four:]], 0))
        conv(z, x3, [(0, 4), (6, 4)], w2, acc, False)
        y_low = (jnp.concatenate([above[two:four].astype(F32), u[0:two]], 0) + acc[0:four]).astype(BF16)
        y_high = (jnp.concatenate([u[full - two :], below[0:two].astype(F32)], 0) + acc[four:eight]).astype(BF16)
        y = jnp.concatenate([y_low, inner[...], y_high], 0).astype(F32)
        goal = jnp.concatenate([above[four:six], target[...], below[four:six]], 0).astype(F32)
        top_grad[...] = zero_rows(z, (y - goal).astype(BF16), 2, 2, top, bottom)
        kept[0:two] = above[two:four]
        kept[two : two + full] = ub
        kept[two + full :] = below[0:two]
        whole_backward(z, kept, top_grad, w1, w2, x3, acc, pre, out_ref, top, bottom)


def other_body(z, fwd, grad, saved, held, above, below, w1, w2, out_ref, x3, acc, pre, kept, top_grad):
    rows, cols = z.rows, z.cols
    two, four, six = 2 * cols, 4 * cols, 6 * cols
    full = rows * cols
    _, decoder, last, top, bottom = roles()

    @pl.when(jnp.logical_not(decoder))
    def _():
        kept[0:two] = above[two:four]
        kept[two : two + full] = saved[...]
        kept[two + full :] = below[two:four]
        top_grad[0:two] = above[four:six]
        top_grad[two : two + full] = block_grad(grad[...], held[...], decoder)
        top_grad[two + full :] = below[four:six]
        whole_backward(z, kept, top_grad, w1, w2, x3, acc, pre, out_ref, top, bottom)

    @pl.when(jnp.logical_and(decoder, jnp.logical_not(last)))
    def _():
        spread(z, x3, 0, above[0:two])
        spread(z, x3, 2, block_input(fwd[...], held[...], decoder).astype(BF16))
        spread(z, x3, 2 + rows, below[0:two])
        conv(z, x3, [(0, rows + 2)], w1, acc, False)
        mid = silu(acc[0 : (rows + 2) * cols]).astype(BF16)
        spread(z, x3, 0, zero_rows(z, mid, 1, 1, top, bottom))
        conv(z, x3, [(0, rows)], w2, acc, False)
        out_ref[...] = (block_input(fwd[...], held[...], decoder) + acc[0:full]).astype(BF16)

    @pl.when(last)
    def _():
        out_ref[...] = jnp.zeros_like(out_ref)


def call(body, z, name, args, outs, scratch, spaces, limit, flops=0, moved=0):
    return pl.pallas_call(
        functools.partial(body, z),
        out_shape=[jax.ShapeDtypeStruct(s, BF16) for s in outs],
        in_specs=[pl.BlockSpec(memory_space=s) for s in spaces],
        out_specs=[pl.BlockSpec(memory_space=pltpu.VMEM) for _ in outs],
        scratch_shapes=scratch,
        compiler_params=pltpu.CompilerParams(vmem_limit_bytes=limit),
        cost_estimate=pl.CostEstimate(flops=flops, bytes_accessed=moved, transcendentals=0),
        name=name,
    )(*args)


def chain_pairs(count):
    half = count // 2
    near, relay, second = [], [], []
    for s in range(half):
        mirror = count - 1 - s
        if s % 2 == 0:
            near += [(s, s + 1), (mirror, mirror - 1)]
        elif s + 1 < half:
            relay += [(mirror, s + 1), (s, mirror - 1)]
        if s >= 1:
            second += [(s, s - 1), (mirror, mirror + 1)]
    return near, relay, second


def on_device(fwd_in, grad_in, saved_in, mirror_held, target, w_first, w_second):
    shape = fwd_in.shape[1:]
    rows, cols, chan = shape
    z = Sizes(rows, cols, chan)
    flat = lambda v: v.reshape(rows * cols, chan)
    fwd, grad, saved, held = (flat(v[0]) for v in (fwd_in, grad_in, saved_in, mirror_held))
    goal = flat(target)
    w1 = w_first[0].reshape(9, chan, chan)
    w2 = w_second[0].reshape(9, chan, chan)
    sections = lax.axis_size("section")
    section, decoder, last, _, _ = roles()
    any_, vm = pl.ANY, pltpu.VMEM
    six = (6 * cols, chan)

    to_up, to_down = call(
        halo_body, z, "halo", (fwd, grad, saved, held, goal), (six, six),
        [pltpu.VMEM((5, 2, 4 * cols, chan), BF16), pltpu.SemaphoreType.DMA((5, 2))],
        [any_] * 5, 8 * MIB,
    )
    count = lax.axis_size("rows")
    below = lax.ppermute(to_up, "rows", [(i + 1, i) for i in range(count - 1)])
    above = lax.ppermute(to_down, "rows", [(i, i + 1) for i in range(count - 1)])

    x3 = pltpu.VMEM(((rows + 4) * cols, 3 * chan), BF16)
    acc = pltpu.VMEM(((rows + 2) * cols, chan), F32)
    wide = pltpu.VMEM(((rows + 4) * cols, chan), BF16)
    row_flops = 2 * cols * 9 * chan * chan
    main, mid = call(
        inner_body, z, "inner", (fwd, grad, saved, held, w1, w2),
        (((rows - 4) * cols, chan), ((rows - 2) * cols, chan)),
        [x3, acc, acc], [vm] * 6, 24 * MIB, 40 * row_flops, 12 * MIB,
    )
    (first,) = call(
        edge_body, z, "edge", (fwd, grad, saved, held, goal, above, below, w1, w2, main, mid),
        ((rows * cols, chan),), [x3, acc, acc, wide, wide], [vm] * 11, 24 * MIB, 24 * row_flops, 12 * MIB,
    )
    near_pairs, relay_pairs, second_pairs = chain_pairs(sections)
    mirrored = lax.ppermute(first, "section", [(s, sections - 1 - s) for s in range(sections)])
    near = lax.ppermute(first, "section", near_pairs)
    (second,) = call(
        other_body, z, "other", (fwd, grad, saved, held, above, below, w1, w2),
        ((rows * cols, chan),), [x3, acc, acc, wide, wide], [vm] * 8, 24 * MIB, 52 * row_flops, 12 * MIB,
    )
    turned = lax.ppermute(second, "section", second_pairs)
    relayed = lax.ppermute(mirrored, "section", relay_pairs)
    half = sections // 2
    onward = jnp.where(section % 2 == (1 - decoder.astype(jnp.int32)), near, relayed)
    inward = jnp.where(jnp.logical_or(section == half, section == half - 1), mirrored, turned)
    fwd_next = jnp.where(decoder, inward, onward)
    grad_next = jnp.where(decoder, onward, inward)
    full = lambda v: v.reshape((1,) + shape)
    return full(fwd_next), full(grad_next), full(mirrored)


def solution(mesh):
    maps = P("section", "rows", None, None)
    weights = P("section", None, None, None, None)
    return jax.shard_map(
        on_device,
        mesh=mesh,
        in_specs=(maps, maps, maps, maps, P("rows", None, None), weights, weights),
        out_specs=(maps, maps, maps),
        check_vma=False,
    )
```

time: 121 us -> 85.2 us (0.70)
  the two profiles are of different devices: /device:TPU:24 before, /device:TPU:18 now
where the time goes in v1:
time: 85.2 us; the launch traced here: 84.5 us
  starting transfers between devices  26.3 us (31%)
  waiting for transfers between devices  24.7 us (29%)
  Pallas kernels  16.8 us (20%)
  local copies, waits for them, and re-layouts  14.8 us (17%)
  other arithmetic  1.08 us (1%)
    pallas_call x4, Pallas kernels, call(): pl.pallas_call(functools.partial(body, z), out_shape=[jax.ShapeDtypeStruc...  16.8 us
    unnamed x27, local copies, waits for them, and re-layouts  14.8 us
    ppermute x1, waiting for transfers between devices, on_device(): lax.ppermute(first, 'section', [(s, sections - 1 - s) for s in range(sect...  13.5 us
    ppermute x1, starting transfers between devices, on_device(): lax.ppermute(first, 'section', [(s, sections - 1 - s) for s in range(sect...  11.4 us
    ppermute x1, waiting for transfers between devices, on_device(): relayed = lax.ppermute(mirrored, 'section', relay_pairs)  6.54 us
    ppermute x1, starting transfers between devices, on_device(): below = lax.ppermute(to_up, 'rows', [(i + 1, i) for i in range(count - 1)])  4.71 us
    ppermute x1, waiting for transfers between devices, on_device(): turned = lax.ppermute(second, 'section', second_pairs)  4.7 us
    ppermute x1, starting transfers between devices, on_device(): lax.ppermute(to_down, 'rows', [(i, i + 1) for i in range(count - 1)])  3.83 us
  transfers between devices with their start and end apart: 6, of which 3 were waited for; matrix products, arithmetic and copies ran while one was open for 0% of the time, Pallas kernels for 15%

profile of v1, /device:TPU:18, one launch (start us, length us, event | category | flops | bytes accessed | tf_op | source)
XLA Modules:
  0.0 84.5 jit_solution(2077634683386633275)
XLA Ops:
  0.6 0.0 copy-start.3
  0.6 1.0 %copy-done.3 = bf16[16,32,512]{2,1,0:T(8,128)(2,1)S(1)} copy-done((bf16[16,32,512]{2,1,0:T(8,128)(2,1)S(1)}, bf16[16,32,512]{2,1,0:T(8,128)(2,1)}, u32[]{:S(2)}) %copy-start.3) | copy-done | bytes 524312
  1.7 0.0 copy-start.5
  1.7 1.0 %copy-done.5 = bf16[1,16,32,512]{3,2,1,0:T(8,128)(2,1)S(1)} copy-done((bf16[1,16,32,512]{3,2,1,0:T(8,128)(2,1)S(1)}, bf16[1,16,32,512]{3,2,1,0:T(8,128)(2,1)}, u32[]{:S(2)}) %copy-start.5) | copy-done | bytes 524312
  2.7 0.0 copy-start.7
  2.7 1.0 %copy-done.7 = bf16[1,16,32,512]{3,2,1,0:T(8,128)(2,1)S(1)} copy-done((bf16[1,16,32,512]{3,2,1,0:T(8,128)(2,1)S(1)}, bf16[1,16,32,512]{3,2,1,0:T(8,128)(2,1)}, u32[]{:S(2)}) %copy-start.7) | copy-done | bytes 524312
  3.8 0.0 copy-start.9
  3.8 1.0 %copy-done.9 = bf16[1,16,32,512]{3,2,1,0:T(8,128)(2,1)S(1)} copy-done((bf16[1,16,32,512]{3,2,1,0:T(8,128)(2,1)S(1)}, bf16[1,16,32,512]{3,2,1,0:T(8,128)(2,1)}, u32[]{:S(2)}) %copy-start.9) | copy-done | bytes 524312
  4.8 0.0 copy-start.11
  4.8 1.0 %copy-done.11 = bf16[1,16,32,512]{3,2,1,0:T(8,128)(2,1)S(1)} copy-done((bf16[1,16,32,512]{3,2,1,0:T(8,128)(2,1)S(1)}, bf16[1,16,32,512]{3,2,1,0:T(8,128)(2,1)}, u32[]{:S(2)}) %copy-start.11) | copy-done | bytes 524312
  5.8 1.9 %halo.1 = (bf16[192,512]{1,0:T(8,128)(2,1)S(1)}, bf16[192,512]{1,0:T(8,128)(2,1)S(1)}) custom-call(bf16[512,512]{1,0:T(8,128)(2,1)S(1)} %bitcast.18, bf16[512,512]{1,0:T(8,128)(2,1)S(1)} %bitcast.22, bf16[512,512]{1,0:T(8,128)(2,1)S(1)} %bitcast.26, bf16[512,512]{1,0:T(8,128)(2,1)S(1)} %bitcast.30, bf16[512,512]{1,0:T(8,128)(2,1)S(1)} %bitcast.16), custom_call_target="tpu_custom_call" | custom-call | tf_op jit(solution)/shard_map/halo/pallas_call | solution.py:279
  7.8 3.8 %collective-permute-start = (bf16[192,512]{1,0:T(8,128)(2,1)S(1)}, bf16[192,512]{1,0:T(8,128)(2,1)S(1)}, u32[]{:S(2)}, u32[]{:S(2)}) collective-permute-start(bf16[192,512]{1,0:T(8,128)(2,1)S(1)} %get-tuple-element.7), channel_id=1, source_target_pairs={{0,1},{1,2},{2,3},{3,4},{4,5},{5,6},{6,7},{7,8},{8,9},{9,10},{10,1... | collective-permute-start | bytes 589832 | tf_op jit(solution)/shard_map/ppermute | solution.py:326
  11.6 4.7 %collective-permute-start.1 = (bf16[192,512]{1,0:T(8,128)(2,1)S(1)}, bf16[192,512]{1,0:T(8,128)(2,1)S(1)}, u32[]{:S(2)}, u32[]{:S(2)}) collective-permute-start(bf16[192,512]{1,0:T(8,128)(2,1)S(1)} %get-tuple-element.8), channel_id=1, source_target_pairs={{1,0},{2,1},{3,2},{4,3},{5,4},{6,5},{7,6},{8,7},{9,8},{10,9},{11,1... | collective-permute-start | bytes 589832 | tf_op jit(solution)/shard_map/ppermute | solution.py:325
  16.3 0.0 copy-start
  16.4 2.3 %copy-done = bf16[1,3,3,512,512]{4,3,2,1,0:T(8,128)(2,1)S(1)} copy-done((bf16[1,3,3,512,512]{4,3,2,1,0:T(8,128)(2,1)S(1)}, bf16[1,3,3,512,512]{4,3,2,1,0:T(8,128)(2,1)}, u32[]{:S(2)}) %copy-start) | copy-done | bytes 4718616
  18.7 0.0 copy-start.2
  18.7 2.3 %copy-done.2 = bf16[1,3,3,512,512]{4,3,2,1,0:T(8,128)(2,1)S(1)} copy-done((bf16[1,3,3,512,512]{4,3,2,1,0:T(8,128)(2,1)S(1)}, bf16[1,3,3,512,512]{4,3,2,1,0:T(8,128)(2,1)}, u32[]{:S(2)}) %copy-start.2) | copy-done | bytes 4718616
  21.0 0.0 copy-start.6
  21.0 1.0 %copy-done.6 = bf16[1,16,32,512]{3,2,1,0:T(8,128)(2,1)S(1)} copy-done((bf16[1,16,32,512]{3,2,1,0:T(8,128)(2,1)S(1)}, bf16[1,16,32,512]{3,2,1,0:T(8,128)(2,1)}, u32[]{:S(2)}) %copy-start.6) | copy-done | bytes 524312
  22.1 0.0 copy-start.8
  22.1 1.0 %copy-done.8 = bf16[1,16,32,512]{3,2,1,0:T(8,128)(2,1)S(1)} copy-done((bf16[1,16,32,512]{3,2,1,0:T(8,128)(2,1)S(1)}, bf16[1,16,32,512]{3,2,1,0:T(8,128)(2,1)}, u32[]{:S(2)}) %copy-start.8) | copy-done | bytes 524312
  23.1 0.0 copy-start.10
  23.1 1.0 %copy-done.10 = bf16[1,16,32,512]{3,2,1,0:T(8,128)(2,1)S(1)} copy-done((bf16[1,16,32,512]{3,2,1,0:T(8,128)(2,1)S(1)}, bf16[1,16,32,512]{3,2,1,0:T(8,128)(2,1)}, u32[]{:S(2)}) %copy-start.10) | copy-done | bytes 524312
  24.1 0.0 copy-start.12
  24.1 1.0 %copy-done.12 = bf16[1,16,32,512]{3,2,1,0:T(8,128)(2,1)S(1)} copy-done((bf16[1,16,32,512]{3,2,1,0:T(8,128)(2,1)S(1)}, bf16[1,16,32,512]{3,2,1,0:T(8,128)(2,1)}, u32[]{:S(2)}) %copy-start.12) | copy-done | bytes 524312
  25.2 0.0 copy-start.1
  25.2 0.0 copy-start.4
  25.2 4.5 %inner.1 = (bf16[384,512]{1,0:T(8,128)(2,1)S(1)}, bf16[448,512]{1,0:T(8,128)(2,1)S(1)}) custom-call(bf16[512,512]{1,0:T(8,128)(2,1)S(1)} %bitcast.19, bf16[512,512]{1,0:T(8,128)(2,1)S(1)} %bitcast.23, bf16[512,512]{1,0:T(8,128)(2,1)S(1)} %bitcast.27, bf16[512,512]{1,0:T(8,128)(2,1)S(1)} %bitcast.31, bf16[9,512,512]{2,1,0:T(8,128)(2,1)S(1)} %bitcast.10, ...), custom_call_target="tpu_custom_call" | custom-call | flops 6039797760 | bytes 12582912 | tf_op jit(solution)/shard_map/inner/pallas_call | solution.py:279
  29.7 0.0 collective-permute-done.above
  29.7 0.0 collective-permute-done.1.below
  29.7 0.0 copy-done.1
  29.7 0.0 copy-done.4
  29.7 1.8 %edge.1 = bf16[512,512]{1,0:T(8,128)(2,1)S(1)} custom-call(bf16[512,512]{1,0:T(8,128)(2,1)S(1)} %bitcast.20, bf16[512,512]{1,0:T(8,128)(2,1)S(1)} %bitcast.24, bf16[512,512]{1,0:T(8,128)(2,1)S(1)} %bitcast.28, bf16[512,512]{1,0:T(8,128)(2,1)S(1)} %bitcast.32, bf16[512,512]{1,0:T(8,128)(2,1)S(1)} %bitcast.17, ...), custom_call_target="tpu_custom_call" | custom-call | flops 3623878656 | bytes 12582912 | tf_op jit(solution)/shard_map/edge/pallas_call | solution.py:279
  31.5 11.4 %collective-permute-start.2 = (bf16[512,512]{1,0:T(8,128)(2,1)S(1)}, bf16[512,512]{1,0:T(8,128)(2,1)S(1)}, u32[]{:S(2)}, u32[]{:S(2)}) collective-permute-start(bf16[512,512]{1,0:T(8,128)(2,1)S(1)} %edge.1), channel_id=1, source_target_pairs={{0,240},{16,224},{32,208},{48,192},{64,176},{80,160},{96,144},{112... | collective-permute-start | bytes 1572872 | tf_op jit(solution)/shard_map/ppermute | solution.py:342
  42.9 3.2 %collective-permute-start.4 = (bf16[512,512]{1,0:T(8,128)(2,1)S(1)}, bf16[512,512]{1,0:T(8,128)(2,1)S(1)}, u32[]{:S(2)}, u32[]{:S(2)}) collective-permute-start(bf16[512,512]{1,0:T(8,128)(2,1)S(1)} %edge.1), channel_id=1, source_target_pairs={{0,16},{240,224},{32,48},{208,192},{64,80},{176,160},{96,112},{144... | collective-permute-start | bytes 1572872 | tf_op jit(solution)/shard_map/ppermute | solution.py:343
  46.1 8.6 %other.1 = bf16[512,512]{1,0:T(8,128)(2,1)S(1)} custom-call(bf16[512,512]{1,0:T(8,128)(2,1)S(1)} %bitcast.21, bf16[512,512]{1,0:T(8,128)(2,1)S(1)} %bitcast.25, bf16[512,512]{1,0:T(8,128)(2,1)S(1)} %bitcast.29, bf16[512,512]{1,0:T(8,128)(2,1)S(1)} %bitcast.33, bf16[192,512]{1,0:T(8,128)(2,1)S(1)} %collective-permute-done.above, ...), custom_call_target="tpu_custom_call" | custom-call | flops 7851737088 | bytes 12582912 | tf_op jit(solution)/shard_map/other/pallas_call | solution.py:279
  54.7 1.9 %collective-permute-start.3 = (bf16[512,512]{1,0:T(8,128)(2,1)S(1)}, bf16[512,512]{1,0:T(8,128)(2,1)S(1)}, u32[]{:S(2)}, u32[]{:S(2)}) collective-permute-start(bf16[512,512]{1,0:T(8,128)(2,1)S(1)} %other.1), channel_id=1, source_target_pairs={{16,0},{224,240},{32,16},{208,224},{48,32},{192,208},{64,48},{176,... | collective-permute-start | bytes 1572872 | tf_op jit(solution)/shard_map/ppermute | solution.py:348
  56.6 13.5 %collective-permute-done.2 = bf16[512,512]{1,0:T(8,128)(2,1)S(1)} collective-permute-done((bf16[512,512]{1,0:T(8,128)(2,1)S(1)}, bf16[512,512]{1,0:T(8,128)(2,1)S(1)}, u32[]{:S(2)}, u32[]{:S(2)}) %collective-permute-start.2) | collective-permute-done | bytes 524320 | tf_op jit(solution)/shard_map/ppermute | solution.py:342
  70.1 1.3 %collective-permute-start.5 = (bf16[512,512]{1,0:T(8,128)(2,1)S(1)}, bf16[512,512]{1,0:T(8,128)(2,1)S(1)}, u32[]{:S(2)}, u32[]{:S(2)}) collective-permute-start(bf16[512,512]{1,0:T(8,128)(2,1)S(1)} %collective-permute-done.2), channel_id=1, source_target_pairs={{224,32},{16,208},{192,64},{48,176},{160,96},{80,144},{225,33},{17... | collective-permute-start | bytes 1572872 | tf_op jit(solution)/shard_map/ppermute | solution.py:349
  71.4 0.0 collective-permute-done.4
  71.4 4.7 %collective-permute-done.3 = bf16[512,512]{1,0:T(8,128)(2,1)S(1)} collective-permute-done((bf16[512,512]{1,0:T(8,128)(2,1)S(1)}, bf16[512,512]{1,0:T(8,128)(2,1)S(1)}, u32[]{:S(2)}, u32[]{:S(2)}) %collective-permute-start.3) | collective-permute-done | bytes 524320 | tf_op jit(solution)/shard_map/ppermute | solution.py:348
  76.1 6.5 %collective-permute-done.5 = bf16[512,512]{1,0:T(8,128)(2,1)S(1)} collective-permute-done((bf16[512,512]{1,0:T(8,128)(2,1)S(1)}, bf16[512,512]{1,0:T(8,128)(2,1)S(1)}, u32[]{:S(2)}, u32[]{:S(2)}) %collective-permute-start.5) | collective-permute-done | bytes 524320 | tf_op jit(solution)/shard_map/ppermute | solution.py:349
  82.6 1.1 %broadcast_select_fusion.2 = (bf16[512,512]{1,0:T(8,128)(2,1)}, bf16[512,512]{1,0:T(8,128)(2,1)}) fusion(pred[]{:T(512)S(6)} %ge.3, bf16[512,512]{1,0:T(8,128)(2,1)S(1)} %collective-permute-done.2, bf16[512,512]{1,0:T(8,128)(2,1)S(1)} %collective-permute-done.3, pred[]{:T(512)S(6)} %or.3, bf16[512,512]{1,0:T(8,128)(2,1)S(1)} %collective-permute-done.4, ...), kind=kLoop, calls=%fused_computation.2 | loop fusion | flops 1048576 | bytes 3145731 | tf_op jit(solution)/shard_map/jit(_where)/select_n | solution.py:354
  83.7 0.8 copy.11
Async XLA Ops:
  0.6 1.0 %copy-start.3 = (bf16[16,32,512]{2,1,0:T(8,128)(2,1)S(1)}, bf16[16,32,512]{2,1,0:T(8,128)(2,1)}, u32[]{:S(2)}) copy-start(bf16[16,32,512]{2,1,0:T(8,128)(2,1)} %param.11) | copy-start | bytes 1572868
  1.7 1.0 %copy-start.5 = (bf16[1,16,32,512]{3,2,1,0:T(8,128)(2,1)S(1)}, bf16[1,16,32,512]{3,2,1,0:T(8,128)(2,1)}, u32[]{:S(2)}) copy-start(bf16[1,16,32,512]{3,2,1,0:T(8,128)(2,1)} %param.7) | copy-start | bytes 1572868
  2.7 1.0 %copy-start.7 = (bf16[1,16,32,512]{3,2,1,0:T(8,128)(2,1)S(1)}, bf16[1,16,32,512]{3,2,1,0:T(8,128)(2,1)}, u32[]{:S(2)}) copy-start(bf16[1,16,32,512]{3,2,1,0:T(8,128)(2,1)} %param.8) | copy-start | bytes 1572868
  3.8 1.0 %copy-start.9 = (bf16[1,16,32,512]{3,2,1,0:T(8,128)(2,1)S(1)}, bf16[1,16,32,512]{3,2,1,0:T(8,128)(2,1)}, u32[]{:S(2)}) copy-start(bf16[1,16,32,512]{3,2,1,0:T(8,128)(2,1)} %param.9) | copy-start | bytes 1572868
  4.8 1.0 %copy-start.11 = (bf16[1,16,32,512]{3,2,1,0:T(8,128)(2,1)S(1)}, bf16[1,16,32,512]{3,2,1,0:T(8,128)(2,1)}, u32[]{:S(2)}) copy-start(bf16[1,16,32,512]{3,2,1,0:T(8,128)(2,1)} %param.10) | copy-start | bytes 1572868
  7.8 21.9 %collective-permute-start = (bf16[192,512]{1,0:T(8,128)(2,1)S(1)}, bf16[192,512]{1,0:T(8,128)(2,1)S(1)}, u32[]{:S(2)}, u32[]{:S(2)}) collective-permute-start(bf16[192,512]{1,0:T(8,128)(2,1)S(1)} %get-tuple-element.7), channel_id=1, source_target_pairs={{0,1},{1,2},{2,3},{3,4},{4,5},{5,6},{6,7},{7,8},{8,9},{9,10},{10,1... | collective-permute-start | bytes 589832 | tf_op jit(solution)/shard_map/ppermute | solution.py:326
  11.6 18.1 %collective-permute-start.1 = (bf16[192,512]{1,0:T(8,128)(2,1)S(1)}, bf16[192,512]{1,0:T(8,128)(2,1)S(1)}, u32[]{:S(2)}, u32[]{:S(2)}) collective-permute-start(bf16[192,512]{1,0:T(8,128)(2,1)S(1)} %get-tuple-element.8), channel_id=1, source_target_pairs={{1,0},{2,1},{3,2},{4,3},{5,4},{6,5},{7,6},{8,7},{9,8},{10,9},{11,1... | collective-permute-start | bytes 589832 | tf_op jit(solution)/shard_map/ppermute | solution.py:325
  16.3 2.3 %copy-start = (bf16[1,3,3,512,512]{4,3,2,1,0:T(8,128)(2,1)S(1)}, bf16[1,3,3,512,512]{4,3,2,1,0:T(8,128)(2,1)}, u32[]{:S(2)}) copy-start(bf16[1,3,3,512,512]{4,3,2,1,0:T(8,128)(2,1)} %param.12) | copy-start | bytes 14155780
  18.7 2.3 %copy-start.2 = (bf16[1,3,3,512,512]{4,3,2,1,0:T(8,128)(2,1)S(1)}, bf16[1,3,3,512,512]{4,3,2,1,0:T(8,128)(2,1)}, u32[]{:S(2)}) copy-start(bf16[1,3,3,512,512]{4,3,2,1,0:T(8,128)(2,1)} %param.13) | copy-start | bytes 14155780
  21.0 1.0 %copy-start.6 = (bf16[1,16,32,512]{3,2,1,0:T(8,128)(2,1)S(1)}, bf16[1,16,32,512]{3,2,1,0:T(8,128)(2,1)}, u32[]{:S(2)}) copy-start(bf16[1,16,32,512]{3,2,1,0:T(8,128)(2,1)} %param.7) | copy-start | bytes 1572868
  22.1 1.0 %copy-start.8 = (bf16[1,16,32,512]{3,2,1,0:T(8,128)(2,1)S(1)}, bf16[1,16,32,512]{3,2,1,0:T(8,128)(2,1)}, u32[]{:S(2)}) copy-start(bf16[1,16,32,512]{3,2,1,0:T(8,128)(2,1)} %param.8) | copy-start | bytes 1572868
  23.1 1.0 %copy-start.10 = (bf16[1,16,32,512]{3,2,1,0:T(8,128)(2,1)S(1)}, bf16[1,16,32,512]{3,2,1,0:T(8,128)(2,1)}, u32[]{:S(2)}) copy-start(bf16[1,16,32,512]{3,2,1,0:T(8,128)(2,1)} %param.9) | copy-start | bytes 1572868
  24.1 1.0 %copy-start.12 = (bf16[1,16,32,512]{3,2,1,0:T(8,128)(2,1)S(1)}, bf16[1,16,32,512]{3,2,1,0:T(8,128)(2,1)}, u32[]{:S(2)}) copy-start(bf16[1,16,32,512]{3,2,1,0:T(8,128)(2,1)} %param.10) | copy-start | bytes 1572868
  25.2 4.5 %copy-start.1 = (bf16[1,3,3,512,512]{4,3,2,1,0:T(8,128)(2,1)S(1)}, bf16[1,3,3,512,512]{4,3,2,1,0:T(8,128)(2,1)}, u32[]{:S(2)}) copy-start(bf16[1,3,3,512,512]{4,3,2,1,0:T(8,128)(2,1)} %param.12) | copy-start | bytes 14155780
  25.2 4.5 %copy-start.4 = (bf16[16,32,512]{2,1,0:T(8,128)(2,1)S(1)}, bf16[16,32,512]{2,1,0:T(8,128)(2,1)}, u32[]{:S(2)}) copy-start(bf16[16,32,512]{2,1,0:T(8,128)(2,1)} %param.11) | copy-start | bytes 1572868
  31.5 38.5 %collective-permute-start.2 = (bf16[512,512]{1,0:T(8,128)(2,1)S(1)}, bf16[512,512]{1,0:T(8,128)(2,1)S(1)}, u32[]{:S(2)}, u32[]{:S(2)}) collective-permute-start(bf16[512,512]{1,0:T(8,128)(2,1)S(1)} %edge.1), channel_id=1, source_target_pairs={{0,240},{16,224},{32,208},{48,192},{64,176},{80,160},{96,144},{112... | collective-permute-start | bytes 1572872 | tf_op jit(solution)/shard_map/ppermute | solution.py:342
  42.9 28.5 %collective-permute-start.4 = (bf16[512,512]{1,0:T(8,128)(2,1)S(1)}, bf16[512,512]{1,0:T(8,128)(2,1)S(1)}, u32[]{:S(2)}, u32[]{:S(2)}) collective-permute-start(bf16[512,512]{1,0:T(8,128)(2,1)S(1)} %edge.1), channel_id=1, source_target_pairs={{0,16},{240,224},{32,48},{208,192},{64,80},{176,160},{96,112},{144... | collective-permute-start | bytes 1572872 | tf_op jit(solution)/shard_map/ppermute | solution.py:343
  54.7 21.4 %collective-permute-start.3 = (bf16[512,512]{1,0:T(8,128)(2,1)S(1)}, bf16[512,512]{1,0:T(8,128)(2,1)S(1)}, u32[]{:S(2)}, u32[]{:S(2)}) collective-permute-start(bf16[512,512]{1,0:T(8,128)(2,1)S(1)} %other.1), channel_id=1, source_target_pairs={{16,0},{224,240},{32,16},{208,224},{48,32},{192,208},{64,48},{176,... | collective-permute-start | bytes 1572872 | tf_op jit(solution)/shard_map/ppermute | solution.py:348
  70.1 12.6 %collective-permute-start.5 = (bf16[512,512]{1,0:T(8,128)(2,1)S(1)}, bf16[512,512]{1,0:T(8,128)(2,1)S(1)}, u32[]{:S(2)}, u32[]{:S(2)}) collective-permute-start(bf16[512,512]{1,0:T(8,128)(2,1)S(1)} %collective-permute-done.2), channel_id=1, source_target_pairs={{224,32},{16,208},{192,64},{48,176},{160,96},{80,144},{225,33},{17... | collective-permute-start | bytes 1572872 | tf_op jit(solution)/shard_map/ppermute | solution.py:349

commit v2 on v1

--- a/solution.py
+++ b/solution.py
@@ -313,13 +313,13 @@
     w2 = w_second[0].reshape(9, chan, chan)
     sections = lax.axis_size("section")
     section, decoder, last, _, _ = roles()
-    any_, vm = pl.ANY, pltpu.VMEM
+    any_, vm = pltpu.HBM, pltpu.VMEM
     six = (6 * cols, chan)
 
     to_up, to_down = call(
-        halo_body, z, "halo", (fwd, grad, saved, held, goal), (six, six),
+        halo_body, z, "halo", tuple(pltpu.with_memory_space_constraint(v, pltpu.HBM) for v in (fwd, grad, saved, held, goal)), (six, six),
         [pltpu.VMEM((5, 2, 4 * cols, chan), BF16), pltpu.SemaphoreType.DMA((5, 2))],
-        [any_] * 5, 8 * MIB,
+        [any_] * 5, 8 * MIB, 6_000_000_000, 0,
     )
     count = lax.axis_size("rows")
     below = lax.ppermute(to_up, "rows", [(i + 1, i) for i in range(count - 1)])

time: 85.2 us -> 73.3 us (0.86)
  local copies, waits for them, and re-layouts: 14.8 us -> 0.82 us
  waiting for transfers between devices: 24.7 us -> 29.5 us
  starting transfers between devices: 26.3 us -> 24.2 us
    unnamed x27 -> x15, local copies, waits for them, and re-layouts: 14.8 us -> 0.82 us
    ppermute x1, waiting for transfers between devices: 0.01 us -> 2.5 us  [on_device(): below = lax.ppermute(to_up, 'rows', [(i + 1, i) for i in range(count - 1)])]
    ppermute x1, waiting for transfers between devices: 13.5 us -> 15.8 us  [on_device(): lax.ppermute(first, 'section', [(s, sections - 1 - s) for s in range(sect...]
    ppermute x1, waiting for transfers between devices: 4.7 us -> 2.4 us  [on_device(): turned = lax.ppermute(second, 'section', second_pairs)]
    ppermute x1, waiting for transfers between devices: 6.54 us -> 8.85 us  [on_device(): relayed = lax.ppermute(mirrored, 'section', relay_pairs)]
    ppermute x1, starting transfers between devices: 11.4 us -> 9.63 us  [on_device(): lax.ppermute(first, 'section', [(s, sections - 1 - s) for s in range(sect...]
  transfers between devices with their start and end apart: 6 -> 6, of which waited for: 3 -> 4; matrix products, arithmetic and copies ran while one was open for 0% -> 0% of each run, Pallas kernels for 15% -> 18%
where the time goes in v2:
time: 73.3 us; the launch traced here: 73.1 us
  waiting for transfers between devices  29.5 us (40%)
  starting transfers between devices  24.2 us (33%)
  Pallas kernels  16.6 us (23%)
  other arithmetic  1.08 us (1%)
  between operations  0.85 us (1%)
  local copies, waits for them, and re-layouts  0.82 us (1%)
    pallas_call x4, Pallas kernels, call(): pl.pallas_call(functools.partial(body, z), out_shape=[jax.ShapeDtypeStruc...  16.6 us
    ppermute x1, waiting for transfers between devices, on_device(): lax.ppermute(first, 'section', [(s, sections - 1 - s) for s in range(sect...  15.8 us
    ppermute x1, starting transfers between devices, on_device(): lax.ppermute(first, 'section', [(s, sections - 1 - s) for s in range(sect...  9.63 us
    ppermute x1, waiting for transfers between devices, on_device(): relayed = lax.ppermute(mirrored, 'section', relay_pairs)  8.85 us
    ppermute x1, starting transfers between devices, on_device(): below = lax.ppermute(to_up, 'rows', [(i + 1, i) for i in range(count - 1)])  4.85 us
    ppermute x1, starting transfers between devices, on_device(): lax.ppermute(to_down, 'rows', [(i, i + 1) for i in range(count - 1)])  4.09 us
    ppermute x1, waiting for transfers between devices, on_device(): below = lax.ppermute(to_up, 'rows', [(i + 1, i) for i in range(count - 1)])  2.5 us
    ppermute x1, starting transfers between devices, on_device(): near = lax.ppermute(first, 'section', near_pairs)  2.42 us
  transfers between devices with their start and end apart: 6, of which 4 were waited for; matrix products, arithmetic and copies ran while one was open for 0% of the time, Pallas kernels for 18%

profile of v2, /device:TPU:18, one launch (start us, length us, event | category | flops | bytes accessed | tf_op | source)
XLA Modules:
  0.0 73.1 jit_solution(10015988467538005503)
XLA Ops:
  0.6 0.0 copy-start
  0.6 0.0 copy-start.1
  0.7 0.0 copy-start.3
  0.7 0.0 copy-start.4
  0.7 0.0 copy-start.5
  0.7 0.0 copy-start.6
  0.7 1.8 %halo.1 = (bf16[192,512]{1,0:T(8,128)(2,1)S(1)}, bf16[192,512]{1,0:T(8,128)(2,1)S(1)}) custom-call(bf16[512,512]{1,0:T(8,128)(2,1)} %bitcast.18, bf16[512,512]{1,0:T(8,128)(2,1)} %bitcast.22, bf16[512,512]{1,0:T(8,128)(2,1)} %bitcast.26, bf16[512,512]{1,0:T(8,128)(2,1)} %bitcast.30, bf16[512,512]{1,0:T(8,128)(2,1)} %bitcast.16), custom_call_target="tpu_custom_call" | custom-call | flops 6000000000 | tf_op jit(solution)/shard_map/halo/pallas_call | solution.py:279
  2.5 4.1 %collective-permute-start = (bf16[192,512]{1,0:T(8,128)(2,1)S(1)}, bf16[192,512]{1,0:T(8,128)(2,1)S(1)}, u32[]{:S(2)}, u32[]{:S(2)}) collective-permute-start(bf16[192,512]{1,0:T(8,128)(2,1)S(1)} %get-tuple-element.7), channel_id=1, source_target_pairs={{0,1},{1,2},{2,3},{3,4},{4,5},{5,6},{6,7},{7,8},{8,9},{9,10},{10,1... | collective-permute-start | bytes 589832 | tf_op jit(solution)/shard_map/ppermute | solution.py:326
  6.6 4.8 %collective-permute-start.1 = (bf16[192,512]{1,0:T(8,128)(2,1)S(1)}, bf16[192,512]{1,0:T(8,128)(2,1)S(1)}, u32[]{:S(2)}, u32[]{:S(2)}) collective-permute-start(bf16[192,512]{1,0:T(8,128)(2,1)S(1)} %get-tuple-element.8), channel_id=1, source_target_pairs={{1,0},{2,1},{3,2},{4,3},{5,4},{6,5},{7,6},{8,7},{9,8},{10,9},{11,1... | collective-permute-start | bytes 589832 | tf_op jit(solution)/shard_map/ppermute | solution.py:325
  11.4 0.0 copy-done
  11.4 0.0 copy-done.1
  11.4 0.0 copy-done.3
  11.4 0.0 copy-done.4
  11.5 0.0 copy-done.5
  11.5 0.0 copy-done.6
  11.5 0.0 copy-start.2
  11.5 4.5 %inner.1 = (bf16[384,512]{1,0:T(8,128)(2,1)S(1)}, bf16[448,512]{1,0:T(8,128)(2,1)S(1)}) custom-call(bf16[512,512]{1,0:T(8,128)(2,1)S(1)} %bitcast.19, bf16[512,512]{1,0:T(8,128)(2,1)S(1)} %bitcast.23, bf16[512,512]{1,0:T(8,128)(2,1)S(1)} %bitcast.27, bf16[512,512]{1,0:T(8,128)(2,1)S(1)} %bitcast.31, bf16[9,512,512]{2,1,0:T(8,128)(2,1)S(1)} %bitcast.10, ...), custom_call_target="tpu_custom_call" | custom-call | flops 6039797760 | bytes 12582912 | tf_op jit(solution)/shard_map/inner/pallas_call | solution.py:279
  16.0 0.0 collective-permute-done.above
  16.0 2.5 %collective-permute-done.1.below = bf16[192,512]{1,0:T(8,128)(2,1)S(1)} collective-permute-done((bf16[192,512]{1,0:T(8,128)(2,1)S(1)}, bf16[192,512]{1,0:T(8,128)(2,1)S(1)}, u32[]{:S(2)}, u32[]{:S(2)}) %collective-permute-start.1) | collective-permute-done | bytes 196640 | tf_op jit(solution)/shard_map/ppermute | solution.py:325
  18.5 0.0 copy-done.2
  18.5 1.8 %edge.1 = bf16[512,512]{1,0:T(8,128)(2,1)S(1)} custom-call(bf16[512,512]{1,0:T(8,128)(2,1)S(1)} %bitcast.20, bf16[512,512]{1,0:T(8,128)(2,1)S(1)} %bitcast.24, bf16[512,512]{1,0:T(8,128)(2,1)S(1)} %bitcast.28, bf16[512,512]{1,0:T(8,128)(2,1)S(1)} %bitcast.32, bf16[512,512]{1,0:T(8,128)(2,1)S(1)} %bitcast.17, ...), custom_call_target="tpu_custom_call" | custom-call | flops 3623878656 | bytes 12582912 | tf_op jit(solution)/shard_map/edge/pallas_call | solution.py:279
  20.3 9.6 %collective-permute-start.2 = (bf16[512,512]{1,0:T(8,128)(2,1)S(1)}, bf16[512,512]{1,0:T(8,128)(2,1)S(1)}, u32[]{:S(2)}, u32[]{:S(2)}) collective-permute-start(bf16[512,512]{1,0:T(8,128)(2,1)S(1)} %edge.1), channel_id=1, source_target_pairs={{0,240},{16,224},{32,208},{48,192},{64,176},{80,160},{96,144},{112... | collective-permute-start | bytes 1572872 | tf_op jit(solution)/shard_map/ppermute | solution.py:342
  29.9 2.4 %collective-permute-start.4 = (bf16[512,512]{1,0:T(8,128)(2,1)S(1)}, bf16[512,512]{1,0:T(8,128)(2,1)S(1)}, u32[]{:S(2)}, u32[]{:S(2)}) collective-permute-start(bf16[512,512]{1,0:T(8,128)(2,1)S(1)} %edge.1), channel_id=1, source_target_pairs={{0,16},{240,224},{32,48},{208,192},{64,80},{176,160},{96,112},{144... | collective-permute-start | bytes 1572872 | tf_op jit(solution)/shard_map/ppermute | solution.py:343
  32.3 8.6 %other.1 = bf16[512,512]{1,0:T(8,128)(2,1)S(1)} custom-call(bf16[512,512]{1,0:T(8,128)(2,1)S(1)} %bitcast.21, bf16[512,512]{1,0:T(8,128)(2,1)S(1)} %bitcast.25, bf16[512,512]{1,0:T(8,128)(2,1)S(1)} %bitcast.29, bf16[512,512]{1,0:T(8,128)(2,1)S(1)} %bitcast.33, bf16[192,512]{1,0:T(8,128)(2,1)S(1)} %collective-permute-done.above, ...), custom_call_target="tpu_custom_call" | custom-call | flops 7851737088 | bytes 12582912 | tf_op jit(solution)/shard_map/other/pallas_call | solution.py:279
  41.0 1.9 %collective-permute-start.3 = (bf16[512,512]{1,0:T(8,128)(2,1)S(1)}, bf16[512,512]{1,0:T(8,128)(2,1)S(1)}, u32[]{:S(2)}, u32[]{:S(2)}) collective-permute-start(bf16[512,512]{1,0:T(8,128)(2,1)S(1)} %other.1), channel_id=1, source_target_pairs={{16,0},{224,240},{32,16},{208,224},{48,32},{192,208},{64,48},{176,... | collective-permute-start | bytes 1572872 | tf_op jit(solution)/shard_map/ppermute | solution.py:348
  42.9 15.8 %collective-permute-done.2 = bf16[512,512]{1,0:T(8,128)(2,1)S(1)} collective-permute-done((bf16[512,512]{1,0:T(8,128)(2,1)S(1)}, bf16[512,512]{1,0:T(8,128)(2,1)S(1)}, u32[]{:S(2)}, u32[]{:S(2)}) %collective-permute-start.2) | collective-permute-done | bytes 524320 | tf_op jit(solution)/shard_map/ppermute | solution.py:342
  58.7 1.3 %collective-permute-start.5 = (bf16[512,512]{1,0:T(8,128)(2,1)S(1)}, bf16[512,512]{1,0:T(8,128)(2,1)S(1)}, u32[]{:S(2)}, u32[]{:S(2)}) collective-permute-start(bf16[512,512]{1,0:T(8,128)(2,1)S(1)} %collective-permute-done.2), channel_id=1, source_target_pairs={{224,32},{16,208},{192,64},{48,176},{160,96},{80,144},{225,33},{17... | collective-permute-start | bytes 1572872 | tf_op jit(solution)/shard_map/ppermute | solution.py:349
  60.0 0.0 collective-permute-done.4
  60.0 2.4 %collective-permute-done.3 = bf16[512,512]{1,0:T(8,128)(2,1)S(1)} collective-permute-done((bf16[512,512]{1,0:T(8,128)(2,1)S(1)}, bf16[512,512]{1,0:T(8,128)(2,1)S(1)}, u32[]{:S(2)}, u32[]{:S(2)}) %collective-permute-start.3) | collective-permute-done | bytes 524320 | tf_op jit(solution)/shard_map/ppermute | solution.py:348
  62.4 8.8 %collective-permute-done.5 = bf16[512,512]{1,0:T(8,128)(2,1)S(1)} collective-permute-done((bf16[512,512]{1,0:T(8,128)(2,1)S(1)}, bf16[512,512]{1,0:T(8,128)(2,1)S(1)}, u32[]{:S(2)}, u32[]{:S(2)}) %collective-permute-start.5) | collective-permute-done | bytes 524320 | tf_op jit(solution)/shard_map/ppermute | solution.py:349
  71.2 1.1 %broadcast_select_fusion.2 = (bf16[512,512]{1,0:T(8,128)(2,1)}, bf16[512,512]{1,0:T(8,128)(2,1)}) fusion(pred[]{:T(512)S(6)} %ge.3, bf16[512,512]{1,0:T(8,128)(2,1)S(1)} %collective-permute-done.2, bf16[512,512]{1,0:T(8,128)(2,1)S(1)} %collective-permute-done.3, pred[]{:T(512)S(6)} %or.3, bf16[512,512]{1,0:T(8,128)(2,1)S(1)} %collective-permute-done.4, ...), kind=kLoop, calls=%fused_computation.2 | loop fusion | flops 1048576 | bytes 3145731 | tf_op jit(solution)/shard_map/jit(_where)/select_n | solution.py:354
  72.3 0.8 %copy.11 = bf16[1,16,32,512]{3,2,1,0:T(8,128)(2,1)} copy(bf16[1,16,32,512]{3,2,1,0:T(8,128)(2,1)S(1)} %bitcast.34) | data formatting | bytes 1048576
Async XLA Ops:
  0.6 10.8 %copy-start = (bf16[1,3,3,512,512]{4,3,2,1,0:T(8,128)(2,1)S(1)}, bf16[1,3,3,512,512]{4,3,2,1,0:T(8,128)(2,1)}, u32[]{:S(2)}) copy-start(bf16[1,3,3,512,512]{4,3,2,1,0:T(8,128)(2,1)} %param.12) | copy-start | bytes 14155780
  0.6 10.8 %copy-start.1 = (bf16[1,3,3,512,512]{4,3,2,1,0:T(8,128)(2,1)S(1)}, bf16[1,3,3,512,512]{4,3,2,1,0:T(8,128)(2,1)}, u32[]{:S(2)}) copy-start(bf16[1,3,3,512,512]{4,3,2,1,0:T(8,128)(2,1)} %param.13) | copy-start | bytes 14155780
  0.7 10.8 %copy-start.3 = (bf16[1,16,32,512]{3,2,1,0:T(8,128)(2,1)S(1)}, bf16[1,16,32,512]{3,2,1,0:T(8,128)(2,1)}, u32[]{:S(2)}) copy-start(bf16[1,16,32,512]{3,2,1,0:T(8,128)(2,1)} %param.7) | copy-start | bytes 1572868
  0.7 10.8 %copy-start.4 = (bf16[1,16,32,512]{3,2,1,0:T(8,128)(2,1)S(1)}, bf16[1,16,32,512]{3,2,1,0:T(8,128)(2,1)}, u32[]{:S(2)}) copy-start(bf16[1,16,32,512]{3,2,1,0:T(8,128)(2,1)} %param.8) | copy-start | bytes 1572868
  0.7 10.8 %copy-start.5 = (bf16[1,16,32,512]{3,2,1,0:T(8,128)(2,1)S(1)}, bf16[1,16,32,512]{3,2,1,0:T(8,128)(2,1)}, u32[]{:S(2)}) copy-start(bf16[1,16,32,512]{3,2,1,0:T(8,128)(2,1)} %param.9) | copy-start | bytes 1572868
  0.7 10.8 %copy-start.6 = (bf16[1,16,32,512]{3,2,1,0:T(8,128)(2,1)S(1)}, bf16[1,16,32,512]{3,2,1,0:T(8,128)(2,1)}, u32[]{:S(2)}) copy-start(bf16[1,16,32,512]{3,2,1,0:T(8,128)(2,1)} %param.10) | copy-start | bytes 1572868
  2.5 13.5 %collective-permute-start = (bf16[192,512]{1,0:T(8,128)(2,1)S(1)}, bf16[192,512]{1,0:T(8,128)(2,1)S(1)}, u32[]{:S(2)}, u32[]{:S(2)}) collective-permute-start(bf16[192,512]{1,0:T(8,128)(2,1)S(1)} %get-tuple-element.7), channel_id=1, source_target_pairs={{0,1},{1,2},{2,3},{3,4},{4,5},{5,6},{6,7},{7,8},{8,9},{9,10},{10,1... | collective-permute-start | bytes 589832 | tf_op jit(solution)/shard_map/ppermute | solution.py:326
  6.6 11.9 %collective-permute-start.1 = (bf16[192,512]{1,0:T(8,128)(2,1)S(1)}, bf16[192,512]{1,0:T(8,128)(2,1)S(1)}, u32[]{:S(2)}, u32[]{:S(2)}) collective-permute-start(bf16[192,512]{1,0:T(8,128)(2,1)S(1)} %get-tuple-element.8), channel_id=1, source_target_pairs={{1,0},{2,1},{3,2},{4,3},{5,4},{6,5},{7,6},{8,7},{9,8},{10,9},{11,1... | collective-permute-start | bytes 589832 | tf_op jit(solution)/shard_map/ppermute | solution.py:325
  11.5 7.0 %copy-start.2 = (bf16[16,32,512]{2,1,0:T(8,128)(2,1)S(1)}, bf16[16,32,512]{2,1,0:T(8,128)(2,1)}, u32[]{:S(2)}) copy-start(bf16[16,32,512]{2,1,0:T(8,128)(2,1)} %param.11) | copy-start | bytes 1572868
  20.3 38.4 %collective-permute-start.2 = (bf16[512,512]{1,0:T(8,128)(2,1)S(1)}, bf16[512,512]{1,0:T(8,128)(2,1)S(1)}, u32[]{:S(2)}, u32[]{:S(2)}) collective-permute-start(bf16[512,512]{1,0:T(8,128)(2,1)S(1)} %edge.1), channel_id=1, source_target_pairs={{0,240},{16,224},{32,208},{48,192},{64,176},{80,160},{96,144},{112... | collective-permute-start | bytes 1572872 | tf_op jit(solution)/shard_map/ppermute | solution.py:342
  29.9 30.1 %collective-permute-start.4 = (bf16[512,512]{1,0:T(8,128)(2,1)S(1)}, bf16[512,512]{1,0:T(8,128)(2,1)S(1)}, u32[]{:S(2)}, u32[]{:S(2)}) collective-permute-start(bf16[512,512]{1,0:T(8,128)(2,1)S(1)} %edge.1), channel_id=1, source_target_pairs={{0,16},{240,224},{32,48},{208,192},{64,80},{176,160},{96,112},{144... | collective-permute-start | bytes 1572872 | tf_op jit(solution)/shard_map/ppermute | solution.py:343
  41.0 21.4 %collective-permute-start.3 = (bf16[512,512]{1,0:T(8,128)(2,1)S(1)}, bf16[512,512]{1,0:T(8,128)(2,1)S(1)}, u32[]{:S(2)}, u32[]{:S(2)}) collective-permute-start(bf16[512,512]{1,0:T(8,128)(2,1)S(1)} %other.1), channel_id=1, source_target_pairs={{16,0},{224,240},{32,16},{208,224},{48,32},{192,208},{64,48},{176,... | collective-permute-start | bytes 1572872 | tf_op jit(solution)/shard_map/ppermute | solution.py:348
  58.7 12.6 %collective-permute-start.5 = (bf16[512,512]{1,0:T(8,128)(2,1)S(1)}, bf16[512,512]{1,0:T(8,128)(2,1)S(1)}, u32[]{:S(2)}, u32[]{:S(2)}) collective-permute-start(bf16[512,512]{1,0:T(8,128)(2,1)S(1)} %collective-permute-done.2), channel_id=1, source_target_pairs={{224,32},{16,208},{192,64},{48,176},{160,96},{80,144},{225,33},{17... | collective-permute-start | bytes 1572872 | tf_op jit(solution)/shard_map/ppermute | solution.py:349

commit v3 on v2

v3 whole, which is shorter than its diff:
```python
import functools

import jax
import jax.numpy as jnp
from jax import lax
from jax.experimental import pallas as pl
from jax.experimental.pallas import tpu as pltpu
from jax.sharding import PartitionSpec as P


BF16 = jnp.bfloat16
F32 = jnp.float32
NN = (((1,), (0,)), ((), ()))
NT = (((1,), (1,)), ((), ()))
MIB = 1 << 20


class Sizes:
    def __init__(self, rows, cols, chan):
        self.rows, self.cols, self.chan = rows, cols, chan


def roles():
    section = lax.axis_index("section")
    sections = lax.axis_size("section")
    row = lax.axis_index("rows")
    decoder = section >= sections // 2
    last = section == sections - 1
    top = row == 0
    bottom = row == lax.axis_size("rows") - 1
    return section, decoder, last, top, bottom


def silu(v):
    return v * jax.nn.sigmoid(v)


def silu_slope(pre):
    sig = jax.nn.sigmoid(pre)
    return sig * (1.0 + pre * (1.0 - sig))


def spread(z, x3, row, value):
    cols, chan = z.cols, z.chan
    count = value.shape[0] // cols
    wide = value.astype(F32).reshape(count, cols, chan)
    col = lax.broadcasted_iota(jnp.int32, wide.shape, 1)
    before = jnp.where(col == 0, 0.0, pltpu.roll(wide, 1, 1))
    after = jnp.where(col == cols - 1, 0.0, pltpu.roll(wide, cols - 1, 1))
    at = slice(row * cols, (row + count) * cols)
    x3[at, 0:chan] = before.reshape(count * cols, chan).astype(BF16)
    x3[at, chan : 2 * chan] = value.astype(BF16)
    x3[at, 2 * chan :] = after.reshape(count * cols, chan).astype(BF16)


def conv(z, x3, pieces, w, acc, flip):
    cols, chan = z.cols, z.chan
    size = sum(n for _, n in pieces) * cols

    def left(a, lanes):
        parts = []
        for start, n in pieces:
            first = (start + a) * cols
            if not isinstance(a, int):
                first = pl.multiple_of(first, cols)
            parts.append(x3[pl.ds(first, n * cols), lanes])
        return parts[0] if len(parts) == 1 else jnp.concatenate(parts, 0)

    def tap_row(a):
        if not flip:
            right = w[pl.ds(3 * a, 3)].reshape(3 * chan, chan)
            return lax.dot_general(left(a, slice(None)), right, NN, preferred_element_type=F32)
        total = None
        for b in range(3):
            right = w[3 * (2 - a) + 2 - b]
            part = lax.dot_general(left(a, slice(b * chan, (b + 1) * chan)), right, NT, preferred_element_type=F32)
            total = part if total is None else total + part
        return total

    for a in range(3):
        if a == 0:
            acc[0:size] = tap_row(0)
        else:
            acc[0:size] += tap_row(a)


def block_input(fwd, held, decoder):
    return fwd.astype(F32) + decoder.astype(F32) * held.astype(F32)


def block_grad(grad, held, decoder):
    return (grad.astype(F32) + (1.0 - decoder.astype(F32)) * held.astype(F32)).astype(BF16)


def halo_body(z, fwd, grad, saved, held, target, up_ref, down_ref, buf, sem):
    rows, cols = z.rows, z.cols
    _, decoder, last, _, _ = roles()
    edge = 4 * cols
    copies = []
    for i, ref in enumerate((fwd, grad, saved, held, target)):
        for e, start in enumerate((0, (rows - 4) * cols)):
            copies.append(pltpu.make_async_copy(ref.at[pl.ds(start, edge)], buf.at[i, e], sem.at[i, e]))
    for c in copies:
        c.start()
    for c in copies:
        c.wait()
    two = 2 * cols
    for e, ref in enumerate((up_ref, down_ref)):
        near = slice(0, two) if e == 0 else slice(two, edge)
        u = block_input(buf[0, e], buf[3, e], decoder).astype(BF16)
        g = block_grad(buf[1, e], buf[3, e], decoder)
        kept = buf[2, e]

        @pl.when(last)
        def _():
            ref[0:edge] = u
            ref[edge:] = buf[4, e][near]

        @pl.when(jnp.logical_not(last))
        def _():
            ref[0:two] = u[near]
            ref[two:edge] = kept[near]
            ref[edge:] = g[near]


def inner_forward(z, fwd, held, w1, w2, main_ref, mid_ref, x3, acc):
    rows, cols = z.rows, z.cols
    _, decoder, last, _, _ = roles()
    m1, m2 = (rows - 2) * cols, (rows - 4) * cols

    @pl.when(jnp.logical_or(jnp.logical_not(decoder), last))
    def _():
        u = block_input(fwd[...], held[...], decoder)
        spread(z, x3, 0, u.astype(BF16))
        conv(z, x3, [(0, rows - 2)], w1, acc, False)
        mid = silu(acc[0:m1]).astype(BF16)
        mid_ref[...] = mid
        spread(z, x3, 0, mid)
        conv(z, x3, [(0, rows - 4)], w2, acc, False)
        keep = slice(2 * cols, (rows - 2) * cols)
        main_ref[...] = (block_input(fwd[keep], held[keep], decoder) + acc[0:m2]).astype(BF16)


def inner_backward(z, grad, saved, held, w1, w2, main_ref, mid_ref, x3, acc, pre):
    rows, cols = z.rows, z.cols
    _, decoder, last, _, _ = roles()
    m1, m2 = (rows - 2) * cols, (rows - 4) * cols

    @pl.when(jnp.logical_and(decoder, jnp.logical_not(last)))
    def _():
        spread(z, x3, 0, saved[...])
        conv(z, x3, [(0, rows - 2)], w1, acc, False)
        pre[0:m1] = acc[0:m1]
        spread(z, x3, 0, block_grad(grad[...], held[...], decoder))
        conv(z, x3, [(0, rows - 2)], w2, acc, True)
        mid = (silu_slope(pre[0:m1]) * acc[0:m1]).astype(BF16)
        mid_ref[...] = mid
        spread(z, x3, 0, mid)
        conv(z, x3, [(0, rows - 4)], w1, acc, True)
        keep = slice(2 * cols, (rows - 2) * cols)
        g = block_grad(grad[keep], held[keep], decoder)
        main_ref[...] = (g.astype(F32) + acc[0:m2]).astype(BF16)


def zero_rows(z, value, lo, hi, top, bottom):
    cols = z.cols
    place = lax.broadcasted_iota(jnp.int32, value.shape, 0)
    outside = jnp.logical_or(
        jnp.logical_and(top, place < lo * cols),
        jnp.logical_and(bottom, place >= value.shape[0] - hi * cols),
    )
    return jnp.where(outside, jnp.zeros_like(value), value)


def whole_backward(z, kept, top_grad, w1, w2, x3, acc, pre, out_ref, top, bottom):
    rows, cols = z.rows, z.cols
    m1, m2 = (rows + 2) * cols, rows * cols
    spread(z, x3, 0, kept[...])
    conv(z, x3, [(0, rows + 2)], w1, acc, False)
    pre[0:m1] = acc[0:m1]
    spread(z, x3, 0, top_grad[...])
    conv(z, x3, [(0, rows + 2)], w2, acc, True)
    mid = (silu_slope(pre[0:m1]) * acc[0:m1]).astype(BF16)
    spread(z, x3, 0, zero_rows(z, mid, 1, 1, top, bottom))
    conv(z, x3, [(0, rows)], w1, acc, True)
    out_ref[...] = (top_grad[2 * cols : 2 * cols + m2].astype(F32) + acc[0:m2]).astype(BF16)


def rest_body(
    z, fwd, grad, saved, held, target, above, below, w1, w2, y_inner, y_mid, g_inner, g_mid,
    first_ref, rim_ref, second_ref, x3, acc, pre, kept, top_grad,
):
    rows, cols = z.rows, z.cols
    two, four, six, eight = 2 * cols, 4 * cols, 6 * cols, 8 * cols
    full = rows * cols
    section, decoder, last, top, bottom = roles()
    encoder = jnp.logical_not(decoder)
    decoder_only = decoder & jnp.logical_not(last)
    closing = last
    m1 = (rows - 2) * cols
    high = slice(full - two, full)

    @pl.when(encoder)
    def _():
        first_ref[two : full - two] = y_inner[...]
        u = block_input(fwd[...], held[...], decoder).astype(BF16)
        spread(z, x3, 0, jnp.concatenate([above[0:two], u[0:two], u[full - two :], below[0:two]], 0))
        conv(z, x3, [(0, 2), (4, 2)], w1, acc, False)
        mid = zero_rows(z, silu(acc[0:four]).astype(BF16), 1, 1, top, bottom)
        spread(z, x3, 0, jnp.concatenate([mid[0:two], y_mid[0:two], y_mid[m1 - two :], mid[two:]], 0))
        conv(z, x3, [(0, 2), (4, 2)], w2, acc, False)
        first_ref[0:two] = (block_input(fwd[0:two], held[0:two], decoder) + acc[0:two]).astype(BF16)
        first_ref[high] = (block_input(fwd[high], held[high], decoder) + acc[two:four]).astype(BF16)
        kept[0:two] = above[two:four]
        kept[two : two + full] = saved[...]
        kept[two + full :] = below[two:four]
        top_grad[0:two] = above[four:six]
        top_grad[two : two + full] = block_grad(grad[...], held[...], decoder)
        top_grad[two + full :] = below[four:six]

    @pl.when(closing)
    def _():
        u = block_input(fwd[...], held[...], decoder)
        ub = u.astype(BF16)
        spread(z, x3, 0, jnp.concatenate([above[0:four], ub[0:two], ub[full - two :], below[0:four]], 0))
        conv(z, x3, [(0, 4), (6, 4)], w1, acc, False)
        mid = zero_rows(z, silu(acc[0:eight]).astype(BF16), 3, 3, top, bottom)
        spread(z, x3, 0, jnp.concatenate([mid[0:four], y_mid[0:two], y_mid[m1 - two :], mid[four:]], 0))
        conv(z, x3, [(0, 4), (6, 4)], w2, acc, False)
        y_low = (jnp.concatenate([above[two:four].astype(F32), u[0:two]], 0) + acc[0:four]).astype(BF16)
        y_high = (jnp.concatenate([u[full - two :], below[0:two].astype(F32)], 0) + acc[four:eight]).astype(BF16)
        y = jnp.concatenate([y_low, y_inner[...], y_high], 0).astype(F32)
        goal = jnp.concatenate([above[four:six], target[...], below[four:six]], 0).astype(F32)
        top_grad[...] = zero_rows(z, (y - goal).astype(BF16), 2, 2, top, bottom)
        kept[0:two] = above[two:four]
        kept[two : two + full] = ub
        kept[two + full :] = below[0:two]

    @pl.when((encoder & (section != 0)) | closing)
    def _():
        whole_backward(z, kept, top_grad, w1, w2, x3, acc, pre, second_ref, top, bottom)

    @pl.when(closing)
    def _():
        first_ref[...] = second_ref[...]

    @pl.when(decoder_only)
    def _():
        first_ref[two : full - two] = g_inner[...]
        spread(z, x3, 0, jnp.concatenate([above[two:four], saved[0:two], saved[high], below[two:four]], 0))
        conv(z, x3, [(0, 2), (4, 2)], w1, acc, False)
        pre[0:four] = acc[0:four]
        g_low = block_grad(grad[0:two], held[0:two], decoder)
        g_high = block_grad(grad[high], held[high], decoder)
        spread(z, x3, 0, jnp.concatenate([above[four:six], g_low, g_high, below[four:six]], 0))
        conv(z, x3, [(0, 2), (4, 2)], w2, acc, True)
        mid = (silu_slope(pre[0:four]) * acc[0:four]).astype(BF16)
        mid = zero_rows(z, mid, 1, 1, top, bottom)
        spread(z, x3, 0, jnp.concatenate([mid[0:two], g_mid[0:two], g_mid[m1 - two :], mid[two:]], 0))
        conv(z, x3, [(0, 2), (4, 2)], w1, acc, True)
        first_ref[0:two] = (g_low.astype(F32) + acc[0:two]).astype(BF16)
        first_ref[high] = (g_high.astype(F32) + acc[two:four]).astype(BF16)

        spread(z, x3, 0, above[0:two])
        spread(z, x3, 2, block_input(fwd[...], held[...], decoder).astype(BF16))
        spread(z, x3, 2 + rows, below[0:two])
        conv(z, x3, [(0, rows + 2)], w1, acc, False)
        hidden = silu(acc[0 : (rows + 2) * cols]).astype(BF16)
        spread(z, x3, 0, zero_rows(z, hidden, 1, 1, top, bottom))
        conv(z, x3, [(0, rows)], w2, acc, False)
        second_ref[...] = (block_input(fwd[...], held[...], decoder) + acc[0:full]).astype(BF16)

    rim_ref[0:two] = first_ref[0:two]
    rim_ref[two:] = first_ref[full - two :]

    @pl.when(section == 1)
    def _():
        first_ref[...] = second_ref[...]


def mirror_body(z, to_decoder, to_encoder, rim, out_ref, sem):
    two, full = 2 * z.cols, z.rows * z.cols
    _, decoder, _, _, _ = roles()
    lower = pltpu.make_async_copy(rim.at[pl.ds(0, two)], out_ref.at[pl.ds(0, two)], sem.at[0])
    upper = pltpu.make_async_copy(rim.at[pl.ds(two, two)], out_ref.at[pl.ds(full - two, two)], sem.at[1])
    lower.start()
    upper.start()
    for here, source in ((decoder, to_decoder), (jnp.logical_not(decoder), to_encoder)):

        @pl.when(here)
        def _():
            copy = pltpu.make_async_copy(source, out_ref.at[pl.ds(two, full - 2 * two)], sem.at[2])
            copy.start()
            copy.wait()

    lower.wait()
    upper.wait()


def pick_body(z, to_decoder, to_encoder, out_ref):
    _, decoder, _, _, _ = roles()

    @pl.when(decoder)
    def _():
        out_ref[...] = to_decoder[...]

    @pl.when(jnp.logical_not(decoder))
    def _():
        out_ref[...] = to_encoder[...]


def finish_body(
    z, near, to_decoder, to_encoder, rim, relay_inner, relay_rim, turned, mirror_in, fwd_ref, grad_ref, mirror_ref, sem
):
    two, full = 2 * z.cols, z.rows * z.cols
    section, decoder, _, _, _ = roles()
    half = lax.axis_size("section") // 2
    plain = section % 2 == 1 - decoder.astype(jnp.int32)
    joined = (section == half) | (section == half - 1)
    first_one = section == 0
    over = jnp.logical_not(joined | first_one)

    def pieces(ref, main, edges, base):
        return [
            pltpu.make_async_copy(main, ref.at[pl.ds(two, full - 2 * two)], sem.at[base]),
            pltpu.make_async_copy(edges.at[pl.ds(0, two)], ref.at[pl.ds(0, two)], sem.at[base + 1]),
            pltpu.make_async_copy(edges.at[pl.ds(two, two)], ref.at[pl.ds(full - two, two)], sem.at[base + 2]),
        ]

    def run(here, copies):
        @pl.when(here)
        def _():
            made = copies()
            for c in made:
                c.start()
            for c in made:
                c.wait()

    for is_decoder in (False, True):
        onward, inward = (grad_ref, fwd_ref) if is_decoder else (fwd_ref, grad_ref)
        inner = to_decoder if is_decoder else to_encoder
        here = decoder == is_decoder
        run(here & plain & joined, lambda: [pltpu.make_async_copy(near, onward, sem.at[0])] + pieces(inward, inner, rim, 3))
        run(here & plain & over, lambda: [pltpu.make_async_copy(near, onward, sem.at[0]), pltpu.make_async_copy(turned, inward, sem.at[3])])
        run(
            here & jnp.logical_not(plain) & over,
            lambda: pieces(onward, relay_inner, relay_rim, 0) + [pltpu.make_async_copy(turned, inward, sem.at[3])],
        )
    run(
        first_one,
        lambda: pieces(fwd_ref, relay_inner, relay_rim, 0)
        + [pltpu.make_async_copy(near, grad_ref, sem.at[3]), pltpu.make_async_copy(turned, mirror_ref, sem.at[4])],
    )


def call(body, z, args, outs, scratch, spaces, limit, flops=0, moved=0, out_space=pltpu.VMEM, aliases=None):
    return pl.pallas_call(
        functools.partial(body, z),
        out_shape=[jax.ShapeDtypeStruct(s, BF16) for s in outs],
        in_specs=[pl.BlockSpec(memory_space=s) for s in spaces],
        out_specs=[pl.BlockSpec(memory_space=out_space) for _ in outs],
        scratch_shapes=scratch,
        input_output_aliases=aliases or {},
        compiler_params=pltpu.CompilerParams(vmem_limit_bytes=limit),
        cost_estimate=pl.CostEstimate(flops=flops, bytes_accessed=moved, transcendentals=0),
    )(*args)


def chain_pairs(count):
    half = count // 2
    near, relay, crossed, turned = [(1, 0)], [], [], [(count - 1, 0)]
    for s in range(half):
        mirror = count - 1 - s
        if s % 2 == 0:
            near += [(s, s + 1), (mirror, mirror - 1)]
            if s > 0:
                crossed += [(s, s - 1), (mirror, mirror + 1)]
        else:
            if s + 1 < half:
                relay += [(mirror, s + 1), (s, mirror - 1)]
            turned += [(s, s - 1), (mirror, mirror + 1)]
    turned.remove((1, 0))
    return near, relay, crossed, turned


def tick(fwd_in, grad_in, saved_in, mirror_held, target, w_first, w_second):
    shape = fwd_in.shape[1:]
    rows, cols, chan = shape
    z = Sizes(rows, cols, chan)
    flat = lambda v: v.reshape(rows * cols, chan)
    fwd, grad, saved, held = (flat(v[0]) for v in (fwd_in, grad_in, saved_in, mirror_held))
    goal = flat(target)
    w1 = w_first[0].reshape(9, chan, chan)
    w2 = w_second[0].reshape(9, chan, chan)
    sections = lax.axis_size("section")
    any_, vm = pltpu.HBM, pltpu.VMEM
    six = (6 * cols, chan)

    to_up, to_down = call(
        halo_body, z, tuple(pltpu.with_memory_space_constraint(v, pltpu.HBM) for v in (fwd, grad, saved, held, goal)), (six, six),
        [pltpu.VMEM((5, 2, 4 * cols, chan), BF16), pltpu.SemaphoreType.DMA((5, 2))],
        [any_] * 5, 8 * MIB, 6_000_000_000, 0,
    )
    count = lax.axis_size("rows")
    above = lax.ppermute(to_down, "rows", [(i, i + 1) for i in range(count - 1)])
    below = lax.ppermute(to_up, "rows", [(i + 1, i) for i in range(count - 1)])

    x3 = pltpu.VMEM(((rows + 4) * cols, 3 * chan), BF16)
    acc = pltpu.VMEM(((rows + 2) * cols, chan), F32)
    wide = pltpu.VMEM(((rows + 4) * cols, chan), BF16)
    row_flops = 2 * cols * 9 * chan * chan
    two, size = 2 * cols, rows * cols
    main_shape, mid_shape = (size - 2 * two, chan), (size - two, chan)
    half = sections // 2
    mirror_pairs = [(s, sections - 1 - s) for s in range(sections)]
    near_pairs, relay_pairs, crossed_pairs, turned_pairs = chain_pairs(sections)
    y_inner, y_mid = call(
        inner_forward, z, (fwd, held, w1, w2), (main_shape, mid_shape),
        [x3, acc], [vm] * 4, 24 * MIB, 26 * row_flops, 12 * MIB,
    )
    to_decoder = lax.ppermute(y_inner, "section", mirror_pairs[:half])
    g_inner, g_mid = call(
        inner_backward, z, (grad, saved, held, w1, w2), (main_shape, mid_shape),
        [x3, acc, acc], [vm] * 5, 24 * MIB, 40 * row_flops, 12 * MIB,
    )
    to_encoder = lax.ppermute(g_inner, "section", mirror_pairs[half:-1])
    operands = (fwd, grad, saved, held, goal, above, below, w1, w2, y_inner, y_mid, g_inner, g_mid)
    results = ((size, chan), (2 * two, chan), (size, chan))
    scratch = [x3, acc, acc, wide, wide]
    first, rim, second = call(rest_body, z, operands, results, scratch, [vm] * 13, 24 * MIB, 70 * row_flops, 12 * MIB)
    mirror_rim = lax.ppermute(rim, "section", [p for p in mirror_pairs if p[1] != 0])
    turned = lax.ppermute(second, "section", crossed_pairs + turned_pairs)
    near = lax.ppermute(first, "section", near_pairs)
    (onward,) = call(pick_body, z, (to_decoder, to_encoder), (main_shape,), [], [vm] * 2, 8 * MIB, 0, MIB)
    relay_inner = lax.ppermute(onward, "section", relay_pairs)
    relay_rim = lax.ppermute(mirror_rim, "section", relay_pairs)
    (mirror_next,) = call(
        mirror_body, z, (to_decoder, to_encoder, mirror_rim), ((size, chan),),
        [pltpu.SemaphoreType.DMA((3,))], [vm] * 3, 8 * MIB, 0, MIB, pltpu.HBM,
    )
    fwd_next, grad_next, mirror_next = call(
        finish_body, z,
        (near, to_decoder, to_encoder, mirror_rim, relay_inner, relay_rim, turned, mirror_next),
        ((size, chan),) * 3, [pltpu.SemaphoreType.DMA((6,))], [vm] * 7 + [pltpu.HBM], 8 * MIB, 0, 2 * MIB, pltpu.HBM,
        aliases={7: 2},
    )
    full = lambda v: v.reshape((1,) + shape)
    return full(fwd_next), full(grad_next), full(mirror_next)


def solution(mesh):
    maps = P("section", "rows", None, None)
    weights = P("section", None, None, None, None)
    return jax.shard_map(
        tick,
        mesh=mesh,
        in_specs=(maps, maps, maps, maps, P("rows", None, None), weights, weights),
        out_specs=(maps, maps, maps),
        check_vma=False,
    )
```

time: 73.3 us -> 75 us (1.023)
  Pallas kernels: 16.6 us -> 18.6 us
  starting transfers between devices: 24.2 us -> 25.9 us
  other arithmetic: 1.08 us -> 0 us
  local copies, waits for them, and re-layouts: 0.82 us -> 0.04 us
    pallas_call x4 -> x7, Pallas kernels: 16.6 us -> 18.6 us  [call(): pl.pallas_call(functools.partial(body, z), out_shape=[jax.ShapeDtypeStruc...]
    ppermute x6 -> x9, starting transfers between devices: 24.2 us -> 25.9 us  [the longest x1 4.71 us: tick(): below = lax.ppermute(to_up, 'rows', [(i + 1, i) for i in range(count - 1)])]
    select_n x1 -> x0, other arithmetic: 1.08 us -> none  [on_device(): grad_next = jnp.where(decoder, onward, inward)]
    unnamed x15 -> x14, local copies, waits for them, and re-layouts: 0.82 us -> 0.04 us
    ppermute x6 -> x9, waiting for transfers between devices: 29.5 us -> 29.1 us  [the longest x1 15.5 us: tick(): lax.ppermute(rim, 'section', [p for p in mirror_pairs if p[1] != 0])]
  transfers between devices with their start and end apart: 6 -> 9, of which waited for: 4 -> 3; matrix products, arithmetic and copies ran while one was open for 0% -> 0% of each run, Pallas kernels for 18% -> 21%
where the time goes in v3:
time: 75 us; the launch traced here: 74.7 us
  waiting for transfers between devices  29.1 us (39%)
  starting transfers between devices  25.9 us (35%)
  Pallas kernels  18.6 us (25%)
  between operations  1.05 us (1%)
    pallas_call x7, Pallas kernels, call(): pl.pallas_call(functools.partial(body, z), out_shape=[jax.ShapeDtypeStruc...  18.6 us
    ppermute x1, waiting for transfers between devices, tick(): lax.ppermute(rim, 'section', [p for p in mirror_pairs if p[1] != 0])  15.5 us
    ppermute x1, waiting for transfers between devices, tick(): to_encoder = lax.ppermute(g_inner, 'section', mirror_pairs[half:-1])  7.28 us
    ppermute x1, waiting for transfers between devices, tick(): relay_rim = lax.ppermute(mirror_rim, 'section', relay_pairs)  6.24 us
    ppermute x1, starting transfers between devices, tick(): below = lax.ppermute(to_up, 'rows', [(i + 1, i) for i in range(count - 1)])  4.71 us
    ppermute x1, starting transfers between devices, tick(): to_decoder = lax.ppermute(y_inner, 'section', mirror_pairs[:half])  4.69 us
    ppermute x1, starting transfers between devices, tick(): lax.ppermute(to_down, 'rows', [(i, i + 1) for i in range(count - 1)])  4.09 us
    ppermute x1, starting transfers between devices, tick(): turned = lax.ppermute(second, 'section', crossed_pairs + turned_pairs)  3.46 us
  transfers between devices with their start and end apart: 9, of which 3 were waited for; matrix products, arithmetic and copies ran while one was open for 0% of the time, Pallas kernels for 21%

profile of v3, /device:TPU:18, one launch (start us, length us, event | category | flops | bytes accessed | tf_op | source)
XLA Modules:
  0.0 74.7 jit_solution(12863041593607791953)
XLA Ops:
  0.6 0.0 copy-start
  0.6 0.0 copy-start.1
  0.7 0.0 copy-start.2
  0.7 0.0 copy-start.5
  0.7 1.8 %shard_map.94 = (bf16[192,512]{1,0:T(8,128)(2,1)S(1)}, bf16[192,512]{1,0:T(8,128)(2,1)S(1)}) custom-call(bf16[512,512]{1,0:T(8,128)(2,1)} %bitcast.16, bf16[512,512]{1,0:T(8,128)(2,1)} %bitcast.19, bf16[512,512]{1,0:T(8,128)(2,1)} %bitcast.22, bf16[512,512]{1,0:T(8,128)(2,1)} %bitcast.25, bf16[512,512]{1,0:T(8,128)(2,1)} %bitcast.29), custom_call_target="tpu_custom_call" | custom-call | flops 6000000000 | tf_op jit(solution)/shard_map/pallas_call | solution.py:357
  2.5 4.1 %collective-permute-start = (bf16[192,512]{1,0:T(8,128)(2,1)S(1)}, bf16[192,512]{1,0:T(8,128)(2,1)S(1)}, u32[]{:S(2)}, u32[]{:S(2)}) collective-permute-start(bf16[192,512]{1,0:T(8,128)(2,1)S(1)} %get-tuple-element.15), channel_id=1, source_target_pairs={{0,1},{1,2},{2,3},{3,4},{4,5},{5,6},{6,7},{7,8},{8,9},{9,10},{10,1... | collective-permute-start | bytes 589832 | tf_op jit(solution)/shard_map/ppermute | solution.py:405
  6.5 4.7 %collective-permute-start.1 = (bf16[192,512]{1,0:T(8,128)(2,1)S(1)}, bf16[192,512]{1,0:T(8,128)(2,1)S(1)}, u32[]{:S(2)}, u32[]{:S(2)}) collective-permute-start(bf16[192,512]{1,0:T(8,128)(2,1)S(1)} %get-tuple-element.16), channel_id=1, source_target_pairs={{1,0},{2,1},{3,2},{4,3},{5,4},{6,5},{7,6},{8,7},{9,8},{10,9},{11,1... | collective-permute-start | bytes 589832 | tf_op jit(solution)/shard_map/ppermute | solution.py:406
  11.3 0.0 copy-done
  11.3 0.0 copy-done.1
  11.3 0.0 copy-done.2
  11.3 0.0 copy-done.5
  11.3 0.0 copy-start.3
  11.3 0.0 copy-start.4
  11.3 4.4 %shard_map.95 = (bf16[384,512]{1,0:T(8,128)(2,1)S(1)}, bf16[448,512]{1,0:T(8,128)(2,1)S(1)}) custom-call(bf16[512,512]{1,0:T(8,128)(2,1)S(1)} %bitcast.17, bf16[512,512]{1,0:T(8,128)(2,1)S(1)} %bitcast.26, bf16[9,512,512]{2,1,0:T(8,128)(2,1)S(1)} %bitcast.10, bf16[9,512,512]{2,1,0:T(8,128)(2,1)S(1)} %bitcast.13), custom_call_target="tpu_custom_call" | custom-call | flops 3925868544 | bytes 12582912 | tf_op jit(solution)/shard_map/pallas_call | solution.py:357
  15.7 0.0 copy-start.6
  15.7 4.7 %collective-permute-start.3 = (bf16[384,512]{1,0:T(8,128)(2,1)S(1)}, bf16[384,512]{1,0:T(8,128)(2,1)S(1)}, u32[]{:S(2)}, u32[]{:S(2)}) collective-permute-start(bf16[384,512]{1,0:T(8,128)(2,1)S(1)} %get-tuple-element.17.y_inner), channel_id=1, source_target_pairs={{0,240},{16,224},{32,208},{48,192},{64,176},{80,160},{96,144},{112... | collective-permute-start | bytes 1179656 | tf_op jit(solution)/shard_map/ppermute | solution.py:421
  20.4 0.0 copy-done.3
  20.4 0.0 copy-done.4
  20.5 1.3 %collective-permute-start.4 = (bf16[384,512]{1,0:T(8,128)(2,1)S(1)}, bf16[384,512]{1,0:T(8,128)(2,1)S(1)}, u32[]{:S(2)}, u32[]{:S(2)}) collective-permute-start(bf16[384,512]{1,0:T(8,128)(2,1)S(1)} %get-tuple-element.19.g_inner), channel_id=1, source_target_pairs={{128,112},{144,96},{160,80},{176,64},{192,48},{208,32},{224,16},{1... | collective-permute-start | bytes 1179656 | tf_op jit(solution)/shard_map/ppermute | solution.py:426
  21.8 0.0 collective-permute-done.above
  21.8 0.0 collective-permute-done.1.below
  21.8 0.0 copy-done.6
  21.8 10.5 %shard_map.97 = (bf16[512,512]{1,0:T(8,128)(2,1)S(1)}, bf16[128,512]{1,0:T(8,128)(2,1)S(1)}, bf16[512,512]{1,0:T(8,128)(2,1)S(1)}) custom-call(bf16[512,512]{1,0:T(8,128)(2,1)S(1)} %bitcast.18, bf16[512,512]{1,0:T(8,128)(2,1)S(1)} %bitcast.21, bf16[512,512]{1,0:T(8,128)(2,1)S(1)} %bitcast.24, bf16[512,512]{1,0:T(8,128)(2,1)S(1)} %bitcast.28, ...), custom_call_target="tpu_custom_call" | custom-call | flops 10569646080 | bytes 12582912 | tf_op jit(solution)/shard_map/pallas_call | solution.py:357
  32.4 3.2 %collective-permute-start.2 = (bf16[512,512]{1,0:T(8,128)(2,1)S(1)}, bf16[512,512]{1,0:T(8,128)(2,1)S(1)}, u32[]{:S(2)}, u32[]{:S(2)}) collective-permute-start(bf16[512,512]{1,0:T(8,128)(2,1)S(1)} %get-tuple-element.21), channel_id=1, source_target_pairs={{16,0},{0,16},{240,224},{32,48},{208,192},{64,80},{176,160},{96,11... | collective-permute-start | bytes 1572872 | tf_op jit(solution)/shard_map/ppermute | solution.py:433
  35.5 3.5 %collective-permute-start.8 = (bf16[512,512]{1,0:T(8,128)(2,1)S(1)}, bf16[512,512]{1,0:T(8,128)(2,1)S(1)}, u32[]{:S(2)}, u32[]{:S(2)}) collective-permute-start(bf16[512,512]{1,0:T(8,128)(2,1)S(1)} %get-tuple-element.23), channel_id=1, source_target_pairs={{32,16},{208,224},{64,48},{176,192},{96,80},{144,160},{240,0},{224... | collective-permute-start | bytes 1572872 | tf_op jit(solution)/shard_map/ppermute | solution.py:432
  39.0 0.0 collective-permute-done.3.to_decoder
  39.0 7.3 %collective-permute-done.4.to_encoder = bf16[384,512]{1,0:T(8,128)(2,1)S(1)} collective-permute-done((bf16[384,512]{1,0:T(8,128)(2,1)S(1)}, bf16[384,512]{1,0:T(8,128)(2,1)S(1)}, u32[]{:S(2)}, u32[]{:S(2)}) %collective-permute-start.4) | collective-permute-done | bytes 393248 | tf_op jit(solution)/shard_map/ppermute | solution.py:426
  46.3 1.3 %collective-permute-start.6 = (bf16[384,512]{1,0:T(8,128)(2,1)S(1)}, bf16[384,512]{1,0:T(8,128)(2,1)S(1)}, u32[]{:S(2)}, u32[]{:S(2)}) collective-permute-start(bf16[384,512]{1,0:T(8,128)(2,1)S(1)} %shard_map.98), channel_id=1, source_target_pairs={{224,32},{16,208},{192,64},{48,176},{160,96},{80,144},{225,33},{17... | collective-permute-start | bytes 1179656 | tf_op jit(solution)/shard_map/ppermute | solution.py:435
  47.6 1.9 %collective-permute-start.5 = (bf16[128,512]{1,0:T(8,128)(2,1)S(1)}, bf16[128,512]{1,0:T(8,128)(2,1)S(1)}, u32[]{:S(2)}, u32[]{:S(2)}) collective-permute-start(bf16[128,512]{1,0:T(8,128)(2,1)S(1)} %get-tuple-element.22), channel_id=1, source_target_pairs={{0,240},{16,224},{32,208},{48,192},{64,176},{80,160},{96,144},{112... | collective-permute-start | bytes 393224 | tf_op jit(solution)/shard_map/ppermute | solution.py:431
  49.5 15.5 %collective-permute-done.5.rim = bf16[128,512]{1,0:T(8,128)(2,1)S(1)} collective-permute-done((bf16[128,512]{1,0:T(8,128)(2,1)S(1)}, bf16[128,512]{1,0:T(8,128)(2,1)S(1)}, u32[]{:S(2)}, u32[]{:S(2)}) %collective-permute-start.5) | collective-permute-done | bytes 131104 | tf_op jit(solution)/shard_map/ppermute | solution.py:431
  65.1 1.3 %collective-permute-start.7 = (bf16[128,512]{1,0:T(8,128)(2,1)S(1)}, bf16[128,512]{1,0:T(8,128)(2,1)S(1)}, u32[]{:S(2)}, u32[]{:S(2)}) collective-permute-start(bf16[128,512]{1,0:T(8,128)(2,1)S(1)} %collective-permute-done.5.rim), channel_id=1, source_target_pairs={{224,32},{16,208},{192,64},{48,176},{160,96},{80,144},{225,33},{17... | collective-permute-start | bytes 393224 | tf_op jit(solution)/shard_map/ppermute | solution.py:436
  66.4 0.8 %shard_map.99.mirror_in = bf16[512,512]{1,0:T(8,128)(2,1)} custom-call(bf16[384,512]{1,0:T(8,128)(2,1)S(1)} %collective-permute-done.3.to_decoder, bf16[384,512]{1,0:T(8,128)(2,1)S(1)} %collective-permute-done.4.to_encoder, bf16[128,512]{1,0:T(8,128)(2,1)S(1)} %collective-permute-done.5.rim), custom_call_target="tpu_custom_call" | custom-call | bytes 1048576 | tf_op jit(solution)/shard_map/pallas_call | solution.py:357
  67.2 6.2 %collective-permute-done.7.relay_rim = bf16[128,512]{1,0:T(8,128)(2,1)S(1)} collective-permute-done((bf16[128,512]{1,0:T(8,128)(2,1)S(1)}, bf16[128,512]{1,0:T(8,128)(2,1)S(1)}, u32[]{:S(2)}, u32[]{:S(2)}) %collective-permute-start.7) | collective-permute-done | bytes 131104 | tf_op jit(solution)/shard_map/ppermute | solution.py:436
  73.4 0.0 collective-permute-done.2.near
  73.4 0.0 collective-permute-done.8.turned
  73.4 0.0 collective-permute-done.6.relay_inner
  73.4 1.1 %shard_map.100 = (bf16[512,512]{1,0:T(8,128)(2,1)}, bf16[512,512]{1,0:T(8,128)(2,1)}, bf16[512,512]{1,0:T(8,128)(2,1)}) custom-call(bf16[512,512]{1,0:T(8,128)(2,1)S(1)} %collective-permute-done.2.near, bf16[384,512]{1,0:T(8,128)(2,1)S(1)} %collective-permute-done.3.to_decoder, ...), custom_call_target="tpu_custom_call", output_to_operand_aliasing={{2}: (7, {})} | custom-call | bytes 2097152 | tf_op jit(solution)/shard_map/pallas_call | solution.py:357
  (2 shorter events, 0.0 us)
Async XLA Ops:
  0.6 10.6 %copy-start = (bf16[1,3,3,512,512]{4,3,2,1,0:T(8,128)(2,1)S(1)}, bf16[1,3,3,512,512]{4,3,2,1,0:T(8,128)(2,1)}, u32[]{:S(2)}) copy-start(bf16[1,3,3,512,512]{4,3,2,1,0:T(8,128)(2,1)} %param.12) | copy-start | bytes 14155780
  0.6 10.6 %copy-start.1 = (bf16[1,3,3,512,512]{4,3,2,1,0:T(8,128)(2,1)S(1)}, bf16[1,3,3,512,512]{4,3,2,1,0:T(8,128)(2,1)}, u32[]{:S(2)}) copy-start(bf16[1,3,3,512,512]{4,3,2,1,0:T(8,128)(2,1)} %param.13) | copy-start | bytes 14155780
  0.7 10.6 %copy-start.2 = (bf16[1,16,32,512]{3,2,1,0:T(8,128)(2,1)S(1)}, bf16[1,16,32,512]{3,2,1,0:T(8,128)(2,1)}, u32[]{:S(2)}) copy-start(bf16[1,16,32,512]{3,2,1,0:T(8,128)(2,1)} %param.7) | copy-start | bytes 1572868
  0.7 10.6 %copy-start.5 = (bf16[1,16,32,512]{3,2,1,0:T(8,128)(2,1)S(1)}, bf16[1,16,32,512]{3,2,1,0:T(8,128)(2,1)}, u32[]{:S(2)}) copy-start(bf16[1,16,32,512]{3,2,1,0:T(8,128)(2,1)} %param.10) | copy-start | bytes 1572868
  2.5 19.3 %collective-permute-start = (bf16[192,512]{1,0:T(8,128)(2,1)S(1)}, bf16[192,512]{1,0:T(8,128)(2,1)S(1)}, u32[]{:S(2)}, u32[]{:S(2)}) collective-permute-start(bf16[192,512]{1,0:T(8,128)(2,1)S(1)} %get-tuple-element.15), channel_id=1, source_target_pairs={{0,1},{1,2},{2,3},{3,4},{4,5},{5,6},{6,7},{7,8},{8,9},{9,10},{10,1... | collective-permute-start | bytes 589832 | tf_op jit(solution)/shard_map/ppermute | solution.py:405
  6.5 15.2 %collective-permute-start.1 = (bf16[192,512]{1,0:T(8,128)(2,1)S(1)}, bf16[192,512]{1,0:T(8,128)(2,1)S(1)}, u32[]{:S(2)}, u32[]{:S(2)}) collective-permute-start(bf16[192,512]{1,0:T(8,128)(2,1)S(1)} %get-tuple-element.16), channel_id=1, source_target_pairs={{1,0},{2,1},{3,2},{4,3},{5,4},{6,5},{7,6},{8,7},{9,8},{10,9},{11,1... | collective-permute-start | bytes 589832 | tf_op jit(solution)/shard_map/ppermute | solution.py:406
  11.3 9.1 %copy-start.3 = (bf16[1,16,32,512]{3,2,1,0:T(8,128)(2,1)S(1)}, bf16[1,16,32,512]{3,2,1,0:T(8,128)(2,1)}, u32[]{:S(2)}) copy-start(bf16[1,16,32,512]{3,2,1,0:T(8,128)(2,1)} %param.8) | copy-start | bytes 1572868
  11.3 9.1 %copy-start.4 = (bf16[1,16,32,512]{3,2,1,0:T(8,128)(2,1)S(1)}, bf16[1,16,32,512]{3,2,1,0:T(8,128)(2,1)}, u32[]{:S(2)}) copy-start(bf16[1,16,32,512]{3,2,1,0:T(8,128)(2,1)} %param.9) | copy-start | bytes 1572868
  15.7 6.1 %copy-start.6 = (bf16[16,32,512]{2,1,0:T(8,128)(2,1)S(1)}, bf16[16,32,512]{2,1,0:T(8,128)(2,1)}, u32[]{:S(2)}) copy-start(bf16[16,32,512]{2,1,0:T(8,128)(2,1)} %param.11) | copy-start | bytes 1572868
  15.7 23.3 %collective-permute-start.3 = (bf16[384,512]{1,0:T(8,128)(2,1)S(1)}, bf16[384,512]{1,0:T(8,128)(2,1)S(1)}, u32[]{:S(2)}, u32[]{:S(2)}) collective-permute-start(bf16[384,512]{1,0:T(8,128)(2,1)S(1)} %get-tuple-element.17.y_inner), channel_id=1, source_target_pairs={{0,240},{16,224},{32,208},{48,192},{64,176},{80,160},{96,144},{112... | collective-permute-start | bytes 1179656 | tf_op jit(solution)/shard_map/ppermute | solution.py:421
  20.5 25.8 %collective-permute-start.4 = (bf16[384,512]{1,0:T(8,128)(2,1)S(1)}, bf16[384,512]{1,0:T(8,128)(2,1)S(1)}, u32[]{:S(2)}, u32[]{:S(2)}) collective-permute-start(bf16[384,512]{1,0:T(8,128)(2,1)S(1)} %get-tuple-element.19.g_inner), channel_id=1, source_target_pairs={{128,112},{144,96},{160,80},{176,64},{192,48},{208,32},{224,16},{1... | collective-permute-start | bytes 1179656 | tf_op jit(solution)/shard_map/ppermute | solution.py:426
  32.4 41.1 %collective-permute-start.2 = (bf16[512,512]{1,0:T(8,128)(2,1)S(1)}, bf16[512,512]{1,0:T(8,128)(2,1)S(1)}, u32[]{:S(2)}, u32[]{:S(2)}) collective-permute-start(bf16[512,512]{1,0:T(8,128)(2,1)S(1)} %get-tuple-element.21), channel_id=1, source_target_pairs={{16,0},{0,16},{240,224},{32,48},{208,192},{64,80},{176,160},{96,11... | collective-permute-start | bytes 1572872 | tf_op jit(solution)/shard_map/ppermute | solution.py:433
  35.5 37.9 %collective-permute-start.8 = (bf16[512,512]{1,0:T(8,128)(2,1)S(1)}, bf16[512,512]{1,0:T(8,128)(2,1)S(1)}, u32[]{:S(2)}, u32[]{:S(2)}) collective-permute-start(bf16[512,512]{1,0:T(8,128)(2,1)S(1)} %get-tuple-element.23), channel_id=1, source_target_pairs={{32,16},{208,224},{64,48},{176,192},{96,80},{144,160},{240,0},{224... | collective-permute-start | bytes 1572872 | tf_op jit(solution)/shard_map/ppermute | solution.py:432
  46.3 27.1 %collective-permute-start.6 = (bf16[384,512]{1,0:T(8,128)(2,1)S(1)}, bf16[384,512]{1,0:T(8,128)(2,1)S(1)}, u32[]{:S(2)}, u32[]{:S(2)}) collective-permute-start(bf16[384,512]{1,0:T(8,128)(2,1)S(1)} %shard_map.98), channel_id=1, source_target_pairs={{224,32},{16,208},{192,64},{48,176},{160,96},{80,144},{225,33},{17... | collective-permute-start | bytes 1179656 | tf_op jit(solution)/shard_map/ppermute | solution.py:435
  47.6 17.5 %collective-permute-start.5 = (bf16[128,512]{1,0:T(8,128)(2,1)S(1)}, bf16[128,512]{1,0:T(8,128)(2,1)S(1)}, u32[]{:S(2)}, u32[]{:S(2)}) collective-permute-start(bf16[128,512]{1,0:T(8,128)(2,1)S(1)} %get-tuple-element.22), channel_id=1, source_target_pairs={{0,240},{16,224},{32,208},{48,192},{64,176},{80,160},{96,144},{112... | collective-permute-start | bytes 393224 | tf_op jit(solution)/shard_map/ppermute | solution.py:431
  65.1 8.4 %collective-permute-start.7 = (bf16[128,512]{1,0:T(8,128)(2,1)S(1)}, bf16[128,512]{1,0:T(8,128)(2,1)S(1)}, u32[]{:S(2)}, u32[]{:S(2)}) collective-permute-start(bf16[128,512]{1,0:T(8,128)(2,1)S(1)} %collective-permute-done.5.rim), channel_id=1, source_target_pairs={{224,32},{16,208},{192,64},{48,176},{160,96},{80,144},{225,33},{17... | collective-permute-start | bytes 393224 | tf_op jit(solution)/shard_map/ppermute | solution.py:436

commit v4 on v3

--- a/solution.py
+++ b/solution.py
@@ -186,21 +186,18 @@
     out_ref[...] = (top_grad[2 * cols : 2 * cols + m2].astype(F32) + acc[0:m2]).astype(BF16)
 
 
-def rest_body(
-    z, fwd, grad, saved, held, target, above, below, w1, w2, y_inner, y_mid, g_inner, g_mid,
-    first_ref, rim_ref, second_ref, x3, acc, pre, kept, top_grad,
+def encoder_rest(
+    z, fwd, grad, saved, held, above, below, w1, w2, y_inner, y_mid, first_in, second_in,
+    first_ref, second_ref, rim_ref, x3, acc, pre, kept, top_grad,
 ):
     rows, cols = z.rows, z.cols
-    two, four, six, eight = 2 * cols, 4 * cols, 6 * cols, 8 * cols
+    two, four, six = 2 * cols, 4 * cols, 6 * cols
     full = rows * cols
-    section, decoder, last, top, bottom = roles()
-    encoder = jnp.logical_not(decoder)
-    decoder_only = decoder & jnp.logical_not(last)
-    closing = last
+    section, decoder, _, top, bottom = roles()
     m1 = (rows - 2) * cols
     high = slice(full - two, full)
 
-    @pl.when(encoder)
+    @pl.when(jnp.logical_not(decoder))
     def _():
         first_ref[two : full - two] = y_inner[...]
         u = block_input(fwd[...], held[...], decoder).astype(BF16)
@@ -217,8 +214,30 @@
         top_grad[0:two] = above[four:six]
         top_grad[two : two + full] = block_grad(grad[...], held[...], decoder)
         top_grad[two + full :] = below[four:six]
-
-    @pl.when(closing)
+        rim_ref[0:two] = first_ref[0:two]
+        rim_ref[two:] = first_ref[full - two :]
+
+    @pl.when(jnp.logical_not(decoder) & (section != 0))
+    def _():
+        whole_backward(z, kept, top_grad, w1, w2, x3, acc, pre, second_ref, top, bottom)
+
+    @pl.when(section == 1)
+    def _():
+        first_ref[...] = second_ref[...]
+
+
+def decoder_rest(
+    z, fwd, grad, saved, held, target, above, below, w1, w2, y_inner, y_mid, g_inner, g_mid,
+    first_ref, second_ref, rim_ref, x3, acc, pre, kept, top_grad,
+):
+    rows, cols = z.rows, z.cols
+    two, four, six, eight = 2 * cols, 4 * cols, 6 * cols, 8 * cols
+    full = rows * cols
+    _, decoder, last, top, bottom = roles()
+    m1 = (rows - 2) * cols
+    high = slice(full - two, full)
+
+    @pl.when(last)
     def _():
         u = block_input(fwd[...], held[...], decoder)
         ub = u.astype(BF16)
@@ -235,16 +254,10 @@
         kept[0:two] = above[two:four]
         kept[two : two + full] = ub
         kept[two + full :] = below[0:two]
-
-    @pl.when((encoder & (section != 0)) | closing)
-    def _():
         whole_backward(z, kept, top_grad, w1, w2, x3, acc, pre, second_ref, top, bottom)
-
-    @pl.when(closing)
-    def _():
         first_ref[...] = second_ref[...]
 
-    @pl.when(decoder_only)
+    @pl.when(decoder & jnp.logical_not(last))
     def _():
         first_ref[two : full - two] = g_inner[...]
         spread(z, x3, 0, jnp.concatenate([above[two:four], saved[0:two], saved[high], below[two:four]], 0))
@@ -270,31 +283,35 @@
         conv(z, x3, [(0, rows)], w2, acc, False)
         second_ref[...] = (block_input(fwd[...], held[...], decoder) + acc[0:full]).astype(BF16)
 
-    rim_ref[0:two] = first_ref[0:two]
-    rim_ref[two:] = first_ref[full - two :]
-
-    @pl.when(section == 1)
-    def _():
-        first_ref[...] = second_ref[...]
-
-
-def mirror_body(z, to_decoder, to_encoder, rim, out_ref, sem):
-    two, full = 2 * z.cols, z.rows * z.cols
+    @pl.when(decoder)
+    def _():
+        rim_ref[0:two] = first_ref[0:two]
+        rim_ref[two:] = first_ref[full - two :]
+
+
+def mirror_body(z, to_decoder, to_encoder, rim_to_decoder, rim_to_encoder, out_ref, sem):
     _, decoder, _, _, _ = roles()
-    lower = pltpu.make_async_copy(rim.at[pl.ds(0, two)], out_ref.at[pl.ds(0, two)], sem.at[0])
-    upper = pltpu.make_async_copy(rim.at[pl.ds(two, two)], out_ref.at[pl.ds(full - two, two)], sem.at[1])
-    lower.start()
-    upper.start()
-    for here, source in ((decoder, to_decoder), (jnp.logical_not(decoder), to_encoder)):
+    for here, inner, rim in (
+        (decoder, to_decoder, rim_to_decoder),
+        (jnp.logical_not(decoder), to_encoder, rim_to_encoder),
+    ):
 
         @pl.when(here)
         def _():
-            copy = pltpu.make_async_copy(source, out_ref.at[pl.ds(two, full - 2 * two)], sem.at[2])
-            copy.start()
-            copy.wait()
-
-    lower.wait()
-    upper.wait()
+            copies = pieces(z, out_ref, inner, rim, sem, 0)
+            for c in copies:
+                c.start()
+            for c in copies:
+                c.wait()
+
+
+def pieces(z, ref, main, edges, sem, base):
+    two, full = 2 * z.cols, z.rows * z.cols
+    return [
+        pltpu.make_async_copy(main, ref.at[pl.ds(two, full - 2 * two)], sem.at[base]),
+        pltpu.make_async_copy(edges.at[pl.ds(0, two)], ref.at[pl.ds(0, two)], sem.at[base + 1]),
+        pltpu.make_async_copy(edges.at[pl.ds(two, two)], ref.at[pl.ds(full - two, two)], sem.at[base + 2]),
+    ]
 
 
 def pick_body(z, to_decoder, to_encoder, out_ref):
@@ -310,22 +327,14 @@
 
 
 def finish_body(
-    z, near, to_decoder, to_encoder, rim, relay_inner, relay_rim, turned, mirror_in, fwd_ref, grad_ref, mirror_ref, sem
+    z, near, to_decoder, to_encoder, rim_to_decoder, rim_to_encoder, relay_inner, relay_rim, turned, mirror_in, fwd_ref, grad_ref, mirror_ref, sem
 ):
-    two, full = 2 * z.cols, z.rows * z.cols
     section, decoder, _, _, _ = roles()
     half = lax.axis_size("section") // 2
     plain = section % 2 == 1 - decoder.astype(jnp.int32)
     joined = (section == half) | (section == half - 1)
     first_one = section == 0
     over = jnp.logical_not(joined | first_one)
-
-    def pieces(ref, main, edges, base):
-        return [
-            pltpu.make_async_copy(main, ref.at[pl.ds(two, full - 2 * two)], sem.at[base]),
-            pltpu.make_async_copy(edges.at[pl.ds(0, two)], ref.at[pl.ds(0, two)], sem.at[base + 1]),
-            pltpu.make_async_copy(edges.at[pl.ds(two, two)], ref.at[pl.ds(full - two, two)], sem.at[base + 2]),
-        ]
 
     def run(here, copies):
         @pl.when(here)
@@ -338,17 +347,17 @@
 
     for is_decoder in (False, True):
         onward, inward = (grad_ref, fwd_ref) if is_decoder else (fwd_ref, grad_ref)
-        inner = to_decoder if is_decoder else to_encoder
+        inner, rim = (to_decoder, rim_to_decoder) if is_decoder else (to_encoder, rim_to_encoder)
         here = decoder == is_decoder
-        run(here & plain & joined, lambda: [pltpu.make_async_copy(near, onward, sem.at[0])] + pieces(inward, inner, rim, 3))
+        run(here & plain & joined, lambda: [pltpu.make_async_copy(near, onward, sem.at[0])] + pieces(z, inward, inner, rim, sem, 3))
         run(here & plain & over, lambda: [pltpu.make_async_copy(near, onward, sem.at[0]), pltpu.make_async_copy(turned, inward, sem.at[3])])
         run(
             here & jnp.logical_not(plain) & over,
-            lambda: pieces(onward, relay_inner, relay_rim, 0) + [pltpu.make_async_copy(turned, inward, sem.at[3])],
+            lambda: pieces(z, onward, relay_inner, relay_rim, sem, 0) + [pltpu.make_async_copy(turned, inward, sem.at[3])],
         )
     run(
         first_one,
-        lambda: pieces(fwd_ref, relay_inner, relay_rim, 0)
+        lambda: pieces(z, fwd_ref, relay_inner, relay_rim, sem, 0)
         + [pltpu.make_async_copy(near, grad_ref, sem.at[3]), pltpu.make_async_copy(turned, mirror_ref, sem.at[4])],
     )
 
@@ -414,35 +423,44 @@
     half = sections // 2
     mirror_pairs = [(s, sections - 1 - s) for s in range(sections)]
     near_pairs, relay_pairs, crossed_pairs, turned_pairs = chain_pairs(sections)
+    g_inner, g_mid = call(
+        inner_backward, z, (grad, saved, held, w1, w2), (main_shape, mid_shape),
+        [x3, acc, acc], [vm] * 5, 24 * MIB, 40 * row_flops, 12 * MIB,
+    )
+    to_encoder = lax.ppermute(g_inner, "section", mirror_pairs[half:-1])
     y_inner, y_mid = call(
         inner_forward, z, (fwd, held, w1, w2), (main_shape, mid_shape),
         [x3, acc], [vm] * 4, 24 * MIB, 26 * row_flops, 12 * MIB,
     )
     to_decoder = lax.ppermute(y_inner, "section", mirror_pairs[:half])
-    g_inner, g_mid = call(
-        inner_backward, z, (grad, saved, held, w1, w2), (main_shape, mid_shape),
-        [x3, acc, acc], [vm] * 5, 24 * MIB, 40 * row_flops, 12 * MIB,
-    )
-    to_encoder = lax.ppermute(g_inner, "section", mirror_pairs[half:-1])
-    operands = (fwd, grad, saved, held, goal, above, below, w1, w2, y_inner, y_mid, g_inner, g_mid)
-    results = ((size, chan), (2 * two, chan), (size, chan))
+    main_args = (fwd, grad, saved, held)
+    whole, rim_shape = (size, chan), (2 * two, chan)
     scratch = [x3, acc, acc, wide, wide]
-    first, rim, second = call(rest_body, z, operands, results, scratch, [vm] * 13, 24 * MIB, 70 * row_flops, 12 * MIB)
-    mirror_rim = lax.ppermute(rim, "section", [p for p in mirror_pairs if p[1] != 0])
+    first, second, rim = call(
+        decoder_rest, z, main_args + (goal, above, below, w1, w2, y_inner, y_mid, g_inner, g_mid),
+        (whole, whole, rim_shape), scratch, [vm] * 13, 24 * MIB, 70 * row_flops, 12 * MIB,
+    )
+    rim_to_encoder = lax.ppermute(rim, "section", mirror_pairs[half:-1])
+    first, second, rim = call(
+        encoder_rest, z, main_args + (above, below, w1, w2, y_inner, y_mid, first, second),
+        (whole, whole, rim_shape), scratch, [vm] * 12, 24 * MIB, 70 * row_flops, 12 * MIB, aliases={10: 0, 11: 1},
+    )
+    rim_to_decoder = lax.ppermute(rim, "section", mirror_pairs[:half])
     turned = lax.ppermute(second, "section", crossed_pairs + turned_pairs)
     near = lax.ppermute(first, "section", near_pairs)
     (onward,) = call(pick_body, z, (to_decoder, to_encoder), (main_shape,), [], [vm] * 2, 8 * MIB, 0, MIB)
     relay_inner = lax.ppermute(onward, "section", relay_pairs)
-    relay_rim = lax.ppermute(mirror_rim, "section", relay_pairs)
+    (onward_rim,) = call(pick_body, z, (rim_to_decoder, rim_to_encoder), (rim_shape,), [], [vm] * 2, 8 * MIB, 0, MIB)
+    relay_rim = lax.ppermute(onward_rim, "section", relay_pairs)
+    arrived = (to_decoder, to_encoder, rim_to_decoder, rim_to_encoder)
     (mirror_next,) = call(
-        mirror_body, z, (to_decoder, to_encoder, mirror_rim), ((size, chan),),
-        [pltpu.SemaphoreType.DMA((3,))], [vm] * 3, 8 * MIB, 0, MIB, pltpu.HBM,
+        mirror_body, z, arrived, (whole,),
+        [pltpu.SemaphoreType.DMA((3,))], [vm] * 4, 8 * MIB, 0, MIB, pltpu.HBM,
     )
     fwd_next, grad_next, mirror_next = call(
-        finish_body, z,
-        (near, to_decoder, to_encoder, mirror_rim, relay_inner, relay_rim, turned, mirror_next),
-        ((size, chan),) * 3, [pltpu.SemaphoreType.DMA((6,))], [vm] * 7 + [pltpu.HBM], 8 * MIB, 0, 2 * MIB, pltpu.HBM,
-        aliases={7: 2},
+        finish_body, z, (near,) + arrived + (relay_inner, relay_rim, turned, mirror_next),
+        (whole,) * 3, [pltpu.SemaphoreType.DMA((6,))], [vm] * 8 + [pltpu.HBM], 8 * MIB, 0, 2 * MIB, pltpu.HBM,
+        aliases={8: 2},
     )
     full = lambda v: v.reshape((1,) + shape)
     return full(fwd_next), full(grad_next), full(mirror_next)

time: 75 us -> 76.9 us (1.025)
  the two profiles are of different devices: /device:TPU:18 before, /device:TPU:2 now
where the time goes in v4:
time: 76.9 us; the launch traced here: 76.6 us
  starting transfers between devices  36.6 us (48%)
  waiting for transfers between devices  19.8 us (26%)
  Pallas kernels  19 us (25%)
  between operations  1.12 us (1%)
    pallas_call x9, Pallas kernels, call(): pl.pallas_call(functools.partial(body, z), out_shape=[jax.ShapeDtypeStruc...  19 us
    ppermute x1, starting transfers between devices, tick(): rim_to_decoder = lax.ppermute(rim, 'section', mirror_pairs[:half])  10.7 us
    ppermute x1, starting transfers between devices, tick(): to_decoder = lax.ppermute(y_inner, 'section', mirror_pairs[:half])  10.4 us
    ppermute x1, waiting for transfers between devices, tick(): rim_to_decoder = lax.ppermute(rim, 'section', mirror_pairs[:half])  9.95 us
    ppermute x1, waiting for transfers between devices, tick(): relay_rim = lax.ppermute(onward_rim, 'section', relay_pairs)  6.24 us
    ppermute x1, starting transfers between devices, tick(): lax.ppermute(to_down, 'rows', [(i, i + 1) for i in range(count - 1)])  4.1 us
    ppermute x1, waiting for transfers between devices, tick(): rim_to_encoder = lax.ppermute(rim, 'section', mirror_pairs[half:-1])  3.61 us
    ppermute x1, starting transfers between devices, tick(): near = lax.ppermute(first, 'section', near_pairs)  2.88 us
  transfers between devices with their start and end apart: 10, of which 3 were waited for; matrix products, arithmetic and copies ran while one was open for 0% of the time, Pallas kernels for 21%

profile of v4, /device:TPU:2, one launch (start us, length us, event | category | flops | bytes accessed | tf_op | source)
XLA Modules:
  0.0 76.6 jit_solution(8854968936454254214)
XLA Ops:
  0.6 0.0 copy-start
  0.6 0.0 copy-start.1
  0.7 0.0 copy-start.4
  0.7 0.0 copy-start.5
  0.7 0.0 copy-start.6
  0.7 1.8 %shard_map.94 = (bf16[192,512]{1,0:T(8,128)(2,1)S(1)}, bf16[192,512]{1,0:T(8,128)(2,1)S(1)}) custom-call(bf16[512,512]{1,0:T(8,128)(2,1)} %bitcast.20, bf16[512,512]{1,0:T(8,128)(2,1)} %bitcast.24, bf16[512,512]{1,0:T(8,128)(2,1)} %bitcast.28, bf16[512,512]{1,0:T(8,128)(2,1)} %bitcast.32, bf16[512,512]{1,0:T(8,128)(2,1)} %bitcast.18), custom_call_target="tpu_custom_call" | custom-call | flops 6000000000 | tf_op jit(solution)/shard_map/pallas_call | solution.py:366
  2.5 4.1 %collective-permute-start = (bf16[192,512]{1,0:T(8,128)(2,1)S(1)}, bf16[192,512]{1,0:T(8,128)(2,1)S(1)}, u32[]{:S(2)}, u32[]{:S(2)}) collective-permute-start(bf16[192,512]{1,0:T(8,128)(2,1)S(1)} %get-tuple-element.18), channel_id=1, source_target_pairs={{0,1},{1,2},{2,3},{3,4},{4,5},{5,6},{6,7},{7,8},{8,9},{9,10},{10,1... | collective-permute-start | bytes 589832 | tf_op jit(solution)/shard_map/ppermute | solution.py:414
  6.6 1.3 %collective-permute-start.1 = (bf16[192,512]{1,0:T(8,128)(2,1)S(1)}, bf16[192,512]{1,0:T(8,128)(2,1)S(1)}, u32[]{:S(2)}, u32[]{:S(2)}) collective-permute-start(bf16[192,512]{1,0:T(8,128)(2,1)S(1)} %get-tuple-element.19), channel_id=1, source_target_pairs={{1,0},{2,1},{3,2},{4,3},{5,4},{6,5},{7,6},{8,7},{9,8},{10,9},{11,1... | collective-permute-start | bytes 589832 | tf_op jit(solution)/shard_map/ppermute | solution.py:415
  7.9 0.0 copy-done
  7.9 0.0 copy-done.1
  7.9 0.0 copy-done.4
  7.9 0.0 copy-done.5
  7.9 0.0 copy-done.6
  7.9 0.0 copy-start.3
  8.0 0.0 copy-start.2
  8.0 1.4 %collective-permute-start.4 = (bf16[384,512]{1,0:T(8,128)(2,1)S(1)}, bf16[384,512]{1,0:T(8,128)(2,1)S(1)}, u32[]{:S(2)}, u32[]{:S(2)}) collective-permute-start(bf16[384,512]{1,0:T(8,128)(2,1)S(1)} %get-tuple-element.22.g_inner), channel_id=1, source_target_pairs={{128,112},{144,96},{160,80},{176,64},{192,48},{208,32},{224,16},{1... | collective-permute-start | bytes 1179656 | tf_op jit(solution)/shard_map/ppermute | solution.py:430
  9.4 0.0 copy-done.3
  9.4 4.4 %shard_map.95 = (bf16[384,512]{1,0:T(8,128)(2,1)S(1)}, bf16[448,512]{1,0:T(8,128)(2,1)S(1)}) custom-call(bf16[512,512]{1,0:T(8,128)(2,1)S(1)} %bitcast.21, bf16[512,512]{1,0:T(8,128)(2,1)S(1)} %bitcast.34, bf16[9,512,512]{2,1,0:T(8,128)(2,1)S(1)} %bitcast.11, bf16[9,512,512]{2,1,0:T(8,128)(2,1)S(1)} %bitcast.15), custom_call_target="tpu_custom_call" | custom-call | flops 3925868544 | bytes 12582912 | tf_op jit(solution)/shard_map/pallas_call | solution.py:366
  13.8 10.4 %collective-permute-start.3 = (bf16[384,512]{1,0:T(8,128)(2,1)S(1)}, bf16[384,512]{1,0:T(8,128)(2,1)S(1)}, u32[]{:S(2)}, u32[]{:S(2)}) collective-permute-start(bf16[384,512]{1,0:T(8,128)(2,1)S(1)} %get-tuple-element.20.y_inner), channel_id=1, source_target_pairs={{0,240},{16,224},{32,208},{48,192},{64,176},{80,160},{96,144},{112... | collective-permute-start | bytes 1179656 | tf_op jit(solution)/shard_map/ppermute | solution.py:435
  24.2 0.0 collective-permute-done.above
  24.2 0.0 collective-permute-done.1.below
  24.2 0.0 copy-done.2
  24.2 0.4 shard_map.97
  24.7 10.5 %shard_map.98 = (bf16[512,512]{1,0:T(8,128)(2,1)S(1)}, bf16[512,512]{1,0:T(8,128)(2,1)S(1)}, bf16[128,512]{1,0:T(8,128)(2,1)S(1)}) custom-call(bf16[512,512]{1,0:T(8,128)(2,1)S(1)} %bitcast.23, bf16[512,512]{1,0:T(8,128)(2,1)S(1)} %bitcast.27, bf16[512,512]{1,0:T(8,128)(2,1)S(1)} %bitcast.31, ...), custom_call_target="tpu_custom_call", output_to_operand_aliasing={{0}: (10, {}), {1}: (11, {})} | custom-call | flops 10569646080 | bytes 12582912 | tf_op jit(solution)/shard_map/pallas_call | solution.py:366
  35.2 2.9 %collective-permute-start.2 = (bf16[512,512]{1,0:T(8,128)(2,1)S(1)}, bf16[512,512]{1,0:T(8,128)(2,1)S(1)}, u32[]{:S(2)}, u32[]{:S(2)}) collective-permute-start(bf16[512,512]{1,0:T(8,128)(2,1)S(1)} %get-tuple-element.26), channel_id=1, source_target_pairs={{16,0},{0,16},{240,224},{32,48},{208,192},{64,80},{176,160},{96,11... | collective-permute-start | bytes 1572872 | tf_op jit(solution)/shard_map/ppermute | solution.py:450
  38.1 1.9 %collective-permute-start.9 = (bf16[512,512]{1,0:T(8,128)(2,1)S(1)}, bf16[512,512]{1,0:T(8,128)(2,1)S(1)}, u32[]{:S(2)}, u32[]{:S(2)}) collective-permute-start(bf16[512,512]{1,0:T(8,128)(2,1)S(1)} %get-tuple-element.29), channel_id=1, source_target_pairs={{32,16},{208,224},{64,48},{176,192},{96,80},{144,160},{240,0},{224... | collective-permute-start | bytes 1572872 | tf_op jit(solution)/shard_map/ppermute | solution.py:449
  40.0 0.0 collective-permute-done.4.to_encoder
  40.0 0.0 collective-permute-done.3.to_decoder
  40.1 1.3 %collective-permute-start.7 = (bf16[384,512]{1,0:T(8,128)(2,1)S(1)}, bf16[384,512]{1,0:T(8,128)(2,1)S(1)}, u32[]{:S(2)}, u32[]{:S(2)}) collective-permute-start(bf16[384,512]{1,0:T(8,128)(2,1)S(1)} %shard_map.99), channel_id=1, source_target_pairs={{224,32},{16,208},{192,64},{48,176},{160,96},{80,144},{225,33},{17... | collective-permute-start | bytes 1179656 | tf_op jit(solution)/shard_map/ppermute | solution.py:452
  41.4 10.7 %collective-permute-start.5 = (bf16[128,512]{1,0:T(8,128)(2,1)S(1)}, bf16[128,512]{1,0:T(8,128)(2,1)S(1)}, u32[]{:S(2)}, u32[]{:S(2)}) collective-permute-start(bf16[128,512]{1,0:T(8,128)(2,1)S(1)} %get-tuple-element.27), channel_id=1, source_target_pairs={{0,240},{16,224},{32,208},{48,192},{64,176},{80,160},{96,144},{112... | collective-permute-start | bytes 393224 | tf_op jit(solution)/shard_map/ppermute | solution.py:448
  52.1 1.3 %collective-permute-start.6 = (bf16[128,512]{1,0:T(8,128)(2,1)S(1)}, bf16[128,512]{1,0:T(8,128)(2,1)S(1)}, u32[]{:S(2)}, u32[]{:S(2)}) collective-permute-start(bf16[128,512]{1,0:T(8,128)(2,1)S(1)} %get-tuple-element.28), channel_id=1, source_target_pairs={{128,112},{144,96},{160,80},{176,64},{192,48},{208,32},{224,16},{1... | collective-permute-start | bytes 393224 | tf_op jit(solution)/shard_map/ppermute | solution.py:443
  53.4 9.9 %collective-permute-done.5.to_decoder.rim_to_decoder = bf16[128,512]{1,0:T(8,128)(2,1)S(1)} collective-permute-done((bf16[128,512]{1,0:T(8,128)(2,1)S(1)}, bf16[128,512]{1,0:T(8,128)(2,1)S(1)}, u32[]{:S(2)}, u32[]{:S(2)}) %collective-permute-start.5) | collective-permute-done | bytes 131104 | tf_op jit(solution)/shard_map/ppermute | solution.py:448
  63.4 3.6 %collective-permute-done.6.to_encoder.rim_to_encoder = bf16[128,512]{1,0:T(8,128)(2,1)S(1)} collective-permute-done((bf16[128,512]{1,0:T(8,128)(2,1)S(1)}, bf16[128,512]{1,0:T(8,128)(2,1)S(1)}, u32[]{:S(2)}, u32[]{:S(2)}) %collective-permute-start.6) | collective-permute-done | bytes 131104 | tf_op jit(solution)/shard_map/ppermute | solution.py:443
  67.0 1.3 %collective-permute-start.8 = (bf16[128,512]{1,0:T(8,128)(2,1)S(1)}, bf16[128,512]{1,0:T(8,128)(2,1)S(1)}, u32[]{:S(2)}, u32[]{:S(2)}) collective-permute-start(bf16[128,512]{1,0:T(8,128)(2,1)S(1)} %shard_map.100), channel_id=1, source_target_pairs={{224,32},{16,208},{192,64},{48,176},{160,96},{80,144},{225,33},{17... | collective-permute-start | bytes 393224 | tf_op jit(solution)/shard_map/ppermute | solution.py:454
  68.3 0.8 %shard_map.101.mirror_in = bf16[512,512]{1,0:T(8,128)(2,1)} custom-call(bf16[384,512]{1,0:T(8,128)(2,1)S(1)} %collective-permute-done.3.to_decoder, bf16[384,512]{1,0:T(8,128)(2,1)S(1)} %collective-permute-done.4.to_encoder, bf16[128,512]{1,0:T(8,128)(2,1)S(1)} %collective-permute-done.5.to_decoder.rim_to_decoder, ...), custom_call_target="tpu_custom_call" | custom-call | bytes 1048576 | tf_op jit(solution)/shard_map/pallas_call | solution.py:366
  69.1 6.2 %collective-permute-done.8.relay_rim = bf16[128,512]{1,0:T(8,128)(2,1)S(1)} collective-permute-done((bf16[128,512]{1,0:T(8,128)(2,1)S(1)}, bf16[128,512]{1,0:T(8,128)(2,1)S(1)}, u32[]{:S(2)}, u32[]{:S(2)}) %collective-permute-start.8) | collective-permute-done | bytes 131104 | tf_op jit(solution)/shard_map/ppermute | solution.py:454
  75.3 0.0 collective-permute-done.2.near
  75.4 0.0 collective-permute-done.9.turned
  75.4 0.0 collective-permute-done.7.relay_inner
  75.4 1.1 %shard_map.102 = (bf16[512,512]{1,0:T(8,128)(2,1)}, bf16[512,512]{1,0:T(8,128)(2,1)}, bf16[512,512]{1,0:T(8,128)(2,1)}) custom-call(bf16[512,512]{1,0:T(8,128)(2,1)S(1)} %collective-permute-done.2.near, bf16[384,512]{1,0:T(8,128)(2,1)S(1)} %collective-permute-done.3.to_decoder, ...), custom_call_target="tpu_custom_call", output_to_operand_aliasing={{2}: (8, {})} | custom-call | bytes 2097152 | tf_op jit(solution)/shard_map/pallas_call | solution.py:366
  (3 shorter events, 0.1 us)
Async XLA Ops:
  0.6 7.2 %copy-start = (bf16[1,3,3,512,512]{4,3,2,1,0:T(8,128)(2,1)S(1)}, bf16[1,3,3,512,512]{4,3,2,1,0:T(8,128)(2,1)}, u32[]{:S(2)}) copy-start(bf16[1,3,3,512,512]{4,3,2,1,0:T(8,128)(2,1)} %param.12) | copy-start | bytes 14155780
  0.6 7.2 %copy-start.1 = (bf16[1,3,3,512,512]{4,3,2,1,0:T(8,128)(2,1)S(1)}, bf16[1,3,3,512,512]{4,3,2,1,0:T(8,128)(2,1)}, u32[]{:S(2)}) copy-start(bf16[1,3,3,512,512]{4,3,2,1,0:T(8,128)(2,1)} %param.13) | copy-start | bytes 14155780
  0.7 7.2 %copy-start.4 = (bf16[1,16,32,512]{3,2,1,0:T(8,128)(2,1)S(1)}, bf16[1,16,32,512]{3,2,1,0:T(8,128)(2,1)}, u32[]{:S(2)}) copy-start(bf16[1,16,32,512]{3,2,1,0:T(8,128)(2,1)} %param.8) | copy-start | bytes 1572868
  0.7 7.2 %copy-start.5 = (bf16[1,16,32,512]{3,2,1,0:T(8,128)(2,1)S(1)}, bf16[1,16,32,512]{3,2,1,0:T(8,128)(2,1)}, u32[]{:S(2)}) copy-start(bf16[1,16,32,512]{3,2,1,0:T(8,128)(2,1)} %param.9) | copy-start | bytes 1572868
  0.7 7.2 %copy-start.6 = (bf16[1,16,32,512]{3,2,1,0:T(8,128)(2,1)S(1)}, bf16[1,16,32,512]{3,2,1,0:T(8,128)(2,1)}, u32[]{:S(2)}) copy-start(bf16[1,16,32,512]{3,2,1,0:T(8,128)(2,1)} %param.10) | copy-start | bytes 1572868
  2.5 21.8 %collective-permute-start = (bf16[192,512]{1,0:T(8,128)(2,1)S(1)}, bf16[192,512]{1,0:T(8,128)(2,1)S(1)}, u32[]{:S(2)}, u32[]{:S(2)}) collective-permute-start(bf16[192,512]{1,0:T(8,128)(2,1)S(1)} %get-tuple-element.18), channel_id=1, source_target_pairs={{0,1},{1,2},{2,3},{3,4},{4,5},{5,6},{6,7},{7,8},{8,9},{9,10},{10,1... | collective-permute-start | bytes 589832 | tf_op jit(solution)/shard_map/ppermute | solution.py:414
  6.6 17.7 %collective-permute-start.1 = (bf16[192,512]{1,0:T(8,128)(2,1)S(1)}, bf16[192,512]{1,0:T(8,128)(2,1)S(1)}, u32[]{:S(2)}, u32[]{:S(2)}) collective-permute-start(bf16[192,512]{1,0:T(8,128)(2,1)S(1)} %get-tuple-element.19), channel_id=1, source_target_pairs={{1,0},{2,1},{3,2},{4,3},{5,4},{6,5},{7,6},{8,7},{9,8},{10,9},{11,1... | collective-permute-start | bytes 589832 | tf_op jit(solution)/shard_map/ppermute | solution.py:415
  7.9 1.5 %copy-start.3 = (bf16[1,16,32,512]{3,2,1,0:T(8,128)(2,1)S(1)}, bf16[1,16,32,512]{3,2,1,0:T(8,128)(2,1)}, u32[]{:S(2)}) copy-start(bf16[1,16,32,512]{3,2,1,0:T(8,128)(2,1)} %param.7) | copy-start | bytes 1572868
  8.0 16.3 %copy-start.2 = (bf16[16,32,512]{2,1,0:T(8,128)(2,1)S(1)}, bf16[16,32,512]{2,1,0:T(8,128)(2,1)}, u32[]{:S(2)}) copy-start(bf16[16,32,512]{2,1,0:T(8,128)(2,1)} %param.11) | copy-start | bytes 1572868
  8.0 32.0 %collective-permute-start.4 = (bf16[384,512]{1,0:T(8,128)(2,1)S(1)}, bf16[384,512]{1,0:T(8,128)(2,1)S(1)}, u32[]{:S(2)}, u32[]{:S(2)}) collective-permute-start(bf16[384,512]{1,0:T(8,128)(2,1)S(1)} %get-tuple-element.22.g_inner), channel_id=1, source_target_pairs={{128,112},{144,96},{160,80},{176,64},{192,48},{208,32},{224,16},{1... | collective-permute-start | bytes 1179656 | tf_op jit(solution)/shard_map/ppermute | solution.py:430
  13.8 26.2 %collective-permute-start.3 = (bf16[384,512]{1,0:T(8,128)(2,1)S(1)}, bf16[384,512]{1,0:T(8,128)(2,1)S(1)}, u32[]{:S(2)}, u32[]{:S(2)}) collective-permute-start(bf16[384,512]{1,0:T(8,128)(2,1)S(1)} %get-tuple-element.20.y_inner), channel_id=1, source_target_pairs={{0,240},{16,224},{32,208},{48,192},{64,176},{80,160},{96,144},{112... | collective-permute-start | bytes 1179656 | tf_op jit(solution)/shard_map/ppermute | solution.py:435
  35.2 40.2 %collective-permute-start.2 = (bf16[512,512]{1,0:T(8,128)(2,1)S(1)}, bf16[512,512]{1,0:T(8,128)(2,1)S(1)}, u32[]{:S(2)}, u32[]{:S(2)}) collective-permute-start(bf16[512,512]{1,0:T(8,128)(2,1)S(1)} %get-tuple-element.26), channel_id=1, source_target_pairs={{16,0},{0,16},{240,224},{32,48},{208,192},{64,80},{176,160},{96,11... | collective-permute-start | bytes 1572872 | tf_op jit(solution)/shard_map/ppermute | solution.py:450
  38.1 37.3 %collective-permute-start.9 = (bf16[512,512]{1,0:T(8,128)(2,1)S(1)}, bf16[512,512]{1,0:T(8,128)(2,1)S(1)}, u32[]{:S(2)}, u32[]{:S(2)}) collective-permute-start(bf16[512,512]{1,0:T(8,128)(2,1)S(1)} %get-tuple-element.29), channel_id=1, source_target_pairs={{32,16},{208,224},{64,48},{176,192},{96,80},{144,160},{240,0},{224... | collective-permute-start | bytes 1572872 | tf_op jit(solution)/shard_map/ppermute | solution.py:449
  40.1 35.3 %collective-permute-start.7 = (bf16[384,512]{1,0:T(8,128)(2,1)S(1)}, bf16[384,512]{1,0:T(8,128)(2,1)S(1)}, u32[]{:S(2)}, u32[]{:S(2)}) collective-permute-start(bf16[384,512]{1,0:T(8,128)(2,1)S(1)} %shard_map.99), channel_id=1, source_target_pairs={{224,32},{16,208},{192,64},{48,176},{160,96},{80,144},{225,33},{17... | collective-permute-start | bytes 1179656 | tf_op jit(solution)/shard_map/ppermute | solution.py:452
  41.4 22.0 %collective-permute-start.5 = (bf16[128,512]{1,0:T(8,128)(2,1)S(1)}, bf16[128,512]{1,0:T(8,128)(2,1)S(1)}, u32[]{:S(2)}, u32[]{:S(2)}) collective-permute-start(bf16[128,512]{1,0:T(8,128)(2,1)S(1)} %get-tuple-element.27), channel_id=1, source_target_pairs={{0,240},{16,224},{32,208},{48,192},{64,176},{80,160},{96,144},{112... | collective-permute-start | bytes 393224 | tf_op jit(solution)/shard_map/ppermute | solution.py:448
  52.1 14.9 %collective-permute-start.6 = (bf16[128,512]{1,0:T(8,128)(2,1)S(1)}, bf16[128,512]{1,0:T(8,128)(2,1)S(1)}, u32[]{:S(2)}, u32[]{:S(2)}) collective-permute-start(bf16[128,512]{1,0:T(8,128)(2,1)S(1)} %get-tuple-element.28), channel_id=1, source_target_pairs={{128,112},{144,96},{160,80},{176,64},{192,48},{208,32},{224,16},{1... | collective-permute-start | bytes 393224 | tf_op jit(solution)/shard_map/ppermute | solution.py:443
  67.0 8.4 %collective-permute-start.8 = (bf16[128,512]{1,0:T(8,128)(2,1)S(1)}, bf16[128,512]{1,0:T(8,128)(2,1)S(1)}, u32[]{:S(2)}, u32[]{:S(2)}) collective-permute-start(bf16[128,512]{1,0:T(8,128)(2,1)S(1)} %shard_map.100), channel_id=1, source_target_pairs={{224,32},{16,208},{192,64},{48,176},{160,96},{80,144},{225,33},{17... | collective-permute-start | bytes 393224 | tf_op jit(solution)/shard_map/ppermute | solution.py:454
